TPU v7x, 32 devices: a whole 2x2x4 slice. The times are simulated.
32 devices in a mesh: bz: 4 (over z), bxy: 8 (over y, x, core).
Axes of the slice: x: 2, y: 2, z: 4, core: 2. Of those that a mesh axis runs over, the one named last changes fastest.
Arguments:
- pdfs: float32 [19, 4, 256, 4096], P(None, None, 'bxy', 'bz'), may hold values from 0.008 to 0.57, as said below
- relax: float32 [4, 256, 4096], P(None, 'bxy', 'bz'), may hold values from 0.6 to 1.9
- fluid: int32 [4, 256, 4096], P(None, 'bxy', 'bz'), may hold values 0 or 1
- targets: int32 [4, 8, 4], P('bz', 'bxy'), may hold values from 0 to 31, as said below
Outputs:
- moved: float32 [19, 4, 256, 4096], P(None, None, 'bxy', 'bz')
Inputs may be any that keep to these rules, and one draw needn't show every extreme that they name: `pdfs`: every entry is positive. Within each row along bz, targets is a permutation of the 32 positions; a block's new owner is its owner or the owner just before or after it along bxy (no wrap), and at most 2 blocks of one owner go to one neighbouring owner.
All inputs are finite; a program needn't handle non-finite values. No bound on the sum of `fluid` on one device may be relied on, other than what follows from the above.
Results may differ from a plain program's by a relative error of at most 0.0003.
Values sent between devices are 32-bit elements; how exact they have to be, the bound alone decides.
A program may use at most 192 MiB of HBM per device.

v0:
```python
import functools

import jax
import jax.numpy as jnp
from jax import lax
from jax.experimental import pallas as pl
from jax.experimental.pallas import tpu as pltpu
from jax.sharding import PartitionSpec as P

MESH = pl.DeviceIdType.MESH
VELOCITIES = (
    (0, 0, 0), (1, 0, 0), (-1, 0, 0), (0, 1, 0), (0, -1, 0), (0, 0, 1), (0, 0, -1),
    (1, 1, 0), (-1, -1, 0), (1, -1, 0), (-1, 1, 0), (1, 0, 1), (-1, 0, -1),
    (1, 0, -1), (-1, 0, 1), (0, 1, 1), (0, -1, -1), (0, 1, -1), (0, -1, 1),
)
OPPOSITE = (0, 2, 1, 4, 3, 6, 5, 8, 7, 10, 9, 12, 11, 14, 13, 16, 15, 18, 17)
Q = 19
ORDER = (5, 11, 14, 15, 18, 6, 12, 13, 16, 17, 0, 1, 2, 3, 4, 7, 8, 9, 10)
AT = tuple(ORDER.index(i) for i in range(Q))
NATURAL = tuple(range(Q))
Y_SENT = tuple(tuple(i for i in range(Q) if VELOCITIES[i][1] == c) for c in (1, -1))
X_SENT = tuple(tuple(i for i in range(Q) if VELOCITIES[i][0] == c) for c in (1, -1))
CORNERS = (7, 8, 9, 10)
SIDE = {1: 0, -1: 1}
VMEM_LIMIT = 60 * 1024 * 1024


def collide(f, rate):
    pair = {i: (f[i] + f[i + 1], f[i] - f[i + 1]) for i in range(1, Q, 2)}
    density = f[0]
    for i in range(1, Q, 2):
        density = density + pair[i][0]
    scale = 3.0 / density
    flow = []
    for axis in range(3):
        total = None
        for i in range(1, Q, 2):
            c = VELOCITIES[i][axis]
            if c:
                d = pair[i][1]
                total = d if total is None else (total + d if c == 1 else total - d)
        flow.append(total * scale)
    base = 1.0 - (flow[0] * flow[0] + flow[1] * flow[1] + flow[2] * flow[2]) * (1.0 / 6.0)
    keep = 1.0 - rate
    drive = rate * density
    post = [None] * Q
    post[0] = keep * f[0] + (drive * (1.0 / 3.0)) * base
    near, far = drive * (1.0 / 18.0), drive * (1.0 / 36.0)
    for i in range(1, Q, 2):
        along = None
        for axis in range(3):
            c = VELOCITIES[i][axis]
            if c:
                along = flow[axis] if along is None else (along + flow[axis] if c == 1 else along - flow[axis])
        even = base + 0.5 * (along * along)
        weight = near if i < 7 else far
        post[i] = keep * f[i] + weight * (even + along)
        post[i + 1] = keep * f[i + 1] + weight * (even - along)
    return post


def collide_block(read, relax_ref, fluid_ref, post_ref):
    rows, width = relax_ref.shape[1:]
    tiles = width // 128

    def body(step, carry):
        r = pl.multiple_of((step // tiles) * 8, 8)
        c = pl.multiple_of((step % tiles) * 128, 128)
        at = (pl.ds(r, 8), pl.ds(c, 128))
        rate = jnp.where(fluid_ref[(0,) + at] > 0, relax_ref[(0,) + at], 0.0)
        post = collide([read(i, at) for i in range(Q)], rate)
        for i in range(Q):
            post_ref[(AT[i], 0) + at] = post[i]
        return carry

    lax.fori_loop(0, (rows // 8) * tiles, body, 0)


def emit_halo(slot, last, edge, post_ref, fluid_ref, ys_ref, xs_ref, cs_ref):
    rows, width = fluid_ref.shape[1:]
    lane = lax.broadcasted_iota(jnp.int32, (rows, 128), 1)
    mine = lane // edge == slot
    for side, first in ((0, width - 128), (1, 0)):
        turn = slot * edge + (edge if side == 0 else 0)
        turn = lax.rem(turn, 128)
        for n in range(6):
            if n < 5:
                tile = post_ref[AT[Y_SENT[side][n]], 0, :, first:first + 128]
            else:
                tile = fluid_ref[0, :, first:first + 128].astype(jnp.float32)
            ys_ref[side, n] = jnp.where(mine, pltpu.roll(tile, turn, 1), ys_ref[side, n])
    for side, row in ((0, rows - 1), (1, 0)):
        for n in range(5):
            xs_ref[side, 0, n:n + 1, :] = post_ref[AT[X_SENT[side][n]], 0, row:row + 1, :]
        xs_ref[side, 0, 5:6, :] = fluid_ref[0, row:row + 1, :].astype(jnp.float32)
        xs_ref[side, 0, 6:8, :] = jnp.zeros((2, width), jnp.float32)

    @pl.when(last)
    def _():
        for k, i in enumerate(CORNERS):
            cx, cy, _z = VELOCITIES[i]
            row = rows - 1 if cx == 1 else 0
            ys = SIDE[cy]
            cs_ref[k, 0:1, :] = ys_ref[ys, Y_SENT[ys].index(i), row:row + 1, :]
            cs_ref[k, 1:2, :] = ys_ref[ys, 5, row:row + 1, :]
            cs_ref[k, 2:8, :] = jnp.zeros((6, 128), jnp.float32)


def first_kernel(edge, pdfs_ref, relax_ref, fluid_ref, post_ref, ys_ref, xs_ref, cs_ref):
    slot = pl.program_id(0)
    collide_block(lambda i, at: pdfs_ref[(i, 0) + at], relax_ref, fluid_ref, post_ref)
    emit_halo(slot, slot == pl.num_programs(0) - 1, edge, post_ref, fluid_ref, ys_ref, xs_ref, cs_ref)


def halo_kernel(ys, xs, cs, yr, xr, cr, send_sem, recv_sem):
    nz, nb = lax.axis_size("bz"), lax.axis_size("bxy")
    z, b = lax.axis_index("bz"), lax.axis_index("bxy")

    def device(dz, db):
        return (lax.rem(z + dz + nz, nz), lax.rem(b + db + nb, nb))

    routes = [(ys.at[0], yr.at[0], 1, 0), (ys.at[1], yr.at[1], -1, 0),
              (xs.at[0], xr.at[0], 0, 1), (xs.at[1], xr.at[1], 0, -1)]
    for k, i in enumerate(CORNERS):
        routes.append((cs.at[k], cr.at[k], VELOCITIES[i][1], VELOCITIES[i][0]))
    barrier = pltpu.get_barrier_semaphore()
    for _s, _d, dz, db in routes:
        pl.semaphore_signal(barrier, inc=1, device_id=device(dz, db), device_id_type=MESH)
    pl.semaphore_wait(barrier, len(routes))
    copies = []
    for n, (src, dst, dz, db) in enumerate(routes):
        copy = pltpu.make_async_remote_copy(
            src_ref=src, dst_ref=dst, send_sem=send_sem.at[n], recv_sem=recv_sem.at[n],
            device_id=device(dz, db), device_id_type=MESH)
        copy.start()
        copies.append(copy)
    for copy in copies:
        copy.wait()


def exchange(ys, xs, cs):
    vmem = pl.BlockSpec(memory_space=pltpu.VMEM)
    return pl.pallas_call(
        halo_kernel,
        out_shape=[jax.ShapeDtypeStruct(a.shape, a.dtype) for a in (ys, xs, cs)],
        in_specs=[vmem] * 3,
        out_specs=[vmem] * 3,
        scratch_shapes=[pltpu.SemaphoreType.DMA((8,)), pltpu.SemaphoreType.DMA((8,))],
        compiler_params=pltpu.CompilerParams(collective_id=0, has_side_effects=True,
                                             vmem_limit_bytes=8 * 1024 * 1024),
        name="halo",
    )(ys, xs, cs)


def lane_shift(velocity, slot, edge, here, below, above, beside):
    _cx, cy, cz = velocity
    width = here.shape[1]
    step = cy * edge + cz
    moved = here if step == 0 else pltpu.roll(here, step % width, 1)
    if cz:
        depth = lax.broadcasted_iota(jnp.int32, here.shape, 1) % edge
        other, face = (below, 0) if cz == 1 else (above, edge - 1)
        carry = step - cz * edge
        wrapped = other if carry == 0 else pltpu.roll(other, carry % width, 1)
        moved = jnp.where(depth == face, wrapped, moved)
    if cy:
        lane = lax.broadcasted_iota(jnp.int32, (here.shape[0], 128), 1)
        offset = 128 if cy == 1 else 256 - edge
        outside = pltpu.roll(beside, lax.rem(offset + cz + 128 - slot * edge, 128), 1)
        if cy == 1:
            moved = jnp.concatenate([jnp.where(lane < edge, outside, moved[:, :128]), moved[:, 128:]], axis=1)
        else:
            moved = jnp.concatenate(
                [moved[:, :-128], jnp.where(lane >= 128 - edge, outside, moved[:, -128:])], axis=1)
    return moved


def arrive(i, slot, edge, slots, here, below, above, yr_ref, xr_ref, cr_ref, fluid):
    velocity = cx, cy, cz = VELOCITIES[i]
    beside = None
    if cy:
        side = SIDE[cy]
        beside = yr_ref[side, 5 if fluid else Y_SENT[side].index(i)]
    moved = lane_shift(velocity, slot, edge, here, below, above, beside)
    if cx:
        side = SIDE[cx]
        row = 5 if fluid else X_SENT[side].index(i)
        rows = moved.shape[0]

        def plane(s):
            return jnp.broadcast_to(xr_ref[side, s, row:row + 1, :], (8, moved.shape[1]))

        corner = None
        if cy:
            k = CORNERS.index(i)
            n = 1 if fluid else 0
            corner = jnp.broadcast_to(cr_ref[k, n:n + 1, :], (8, 128))
        entering = lane_shift(
            velocity, slot, edge, plane(slot), plane(jnp.maximum(slot - 1, 0)) if cz == 1 else None,
            plane(jnp.minimum(slot + 1, slots - 1)) if cz == -1 else None, corner)
        index = lax.broadcasted_iota(jnp.int32, (8, moved.shape[1]), 0)
        moved = pltpu.roll(moved, cx % rows, 0)
        if cx == 1:
            moved = jnp.concatenate([jnp.where(index == 0, entering, moved[:8]), moved[8:]], axis=0)
        else:
            moved = jnp.concatenate([moved[:-8], jnp.where(index == 7, entering, moved[-8:])], axis=0)
    return moved


def stream_block(slot, edge, slots, mask_ref, post_ref, below_ref, above_ref, yr_ref, xr_ref, cr_ref, write):
    for i in range(Q):
        cz = VELOCITIES[i][2]
        own = post_ref[AT[i], 0]
        if i == 0:
            write(0, own)
            continue
        value = arrive(
            i, slot, edge, slots, own, below_ref[AT[i], 0] if cz == 1 else None,
            above_ref[AT[i] - 5, 0] if cz == -1 else None, yr_ref, xr_ref, cr_ref, False)
        mask = mask_ref[0]
        stay = jnp.where(mask > 0, post_ref[AT[OPPOSITE[i]], 0], own)
        write(i, jnp.where((mask & (1 << i)) != 0, value, stay))


def middle_kernel(edge, ends_ref, post_ref, below_ref, above_ref, relax_ref, fluid_ref, fbelow_ref, fabove_ref,
                  yr_ref, xr_ref, cr_ref, out_ref, mask_ref, ys_ref, xs_ref, cs_ref, next_ref):
    slot, slots = pl.program_id(0), pl.num_programs(0)
    rows, width = fluid_ref.shape[1:]
    row = lax.broadcasted_iota(jnp.int32, (rows, width), 0)
    lane = lax.broadcasted_iota(jnp.int32, (rows, width), 1)
    depth = lane % edge
    fluid = fluid_ref[0].astype(jnp.float32)
    bits = jnp.ones((rows, width), jnp.int32)
    for i in range(1, Q):
        cx, cy, cz = VELOCITIES[i]
        source = arrive(i, slot, edge, slots, fluid, fbelow_ref[0].astype(jnp.float32) if cz == 1 else None,
                        fabove_ref[0].astype(jnp.float32) if cz == -1 else None, yr_ref, xr_ref, cr_ref, True)
        bit = jnp.where(source > 0.5, 1 << i, 0)
        if cx:
            edge_row = 0 if cx == 1 else rows - 1
            bit = jnp.where((row == edge_row) & (ends_ref[0 if cx == 1 else 1] > 0), 0, bit)
        if cy:
            outer = lane < edge if cy == 1 else lane >= width - edge
            bit = jnp.where(outer & (ends_ref[2 if cy == 1 else 3] > 0), 0, bit)
        if cz:
            final = 0 if cz == 1 else slots - 1
            face = 0 if cz == 1 else edge - 1
            bit = jnp.where((depth == face) & (slot == final), 0, bit)
        bits = bits | bit
    mask_ref[0] = jnp.where(fluid_ref[0] > 0, bits, 0)

    def write(i, value):
        next_ref[i] = value

    stream_block(slot, edge, slots, mask_ref, post_ref, below_ref, above_ref, yr_ref, xr_ref, cr_ref, write)
    collide_block(lambda i, at: next_ref[(i,) + at], relax_ref, fluid_ref, out_ref)
    emit_halo(slot, slot == slots - 1, edge, out_ref, fluid_ref, ys_ref, xs_ref, cs_ref)


def last_kernel(edge, mask_ref, post_ref, below_ref, above_ref, yr_ref, xr_ref, cr_ref, out_ref):
    def write(i, value):
        out_ref[i, 0] = value

    stream_block(pl.program_id(0), edge, pl.num_programs(0), mask_ref, post_ref, below_ref, above_ref,
                 yr_ref, xr_ref, cr_ref, write)


def pack_kernel(pick_ref, source_ref, out_ref):
    out_ref[...] = source_ref[...]


def pack(final, pick):
    q, _blocks, rows, width = final.shape
    count = pick.shape[0]
    parts = 2 if rows % 16 == 0 else 1
    block = (q, 1, rows // parts, width)
    return pl.pallas_call(
        pack_kernel,
        out_shape=jax.ShapeDtypeStruct((q, count, rows, width), final.dtype),
        grid_spec=pltpu.PrefetchScalarGridSpec(
            num_scalar_prefetch=1, grid=(count, parts),
            in_specs=[pl.BlockSpec(block, lambda g, h, pick: (0, pick[g], h, 0))],
            out_specs=pl.BlockSpec(block, lambda g, h, pick: (0, g, h, 0))),
        compiler_params=pltpu.CompilerParams(vmem_limit_bytes=VMEM_LIMIT),
        name="pack",
    )(pick, final)


def place_kernel(table_ref, final_ref, left_ref, right_ref, out_ref):
    kind = table_ref[pl.program_id(0), 0]

    @pl.when(kind == 0)
    def _():
        out_ref[...] = final_ref[...]

    @pl.when(kind == 1)
    def _():
        out_ref[...] = left_ref[...]

    @pl.when(kind == 2)
    def _():
        out_ref[...] = right_ref[...]


def place(final, left, right, table):
    q, blocks, rows, width = final.shape
    parts = 2 if rows % 16 == 0 else 1
    block = (q, 1, rows // parts, width)

    def taken(kind):
        def index(k, h, table):
            used = table[k, 0] == kind
            return (0, jnp.where(used, table[k, 1], 0), jnp.where(used, h, 0), 0)
        return pl.BlockSpec(block, index)

    return pl.pallas_call(
        place_kernel,
        out_shape=jax.ShapeDtypeStruct(final.shape, final.dtype),
        grid_spec=pltpu.PrefetchScalarGridSpec(
            num_scalar_prefetch=1, grid=(blocks, parts),
            in_specs=[taken(0), taken(1), taken(2)],
            out_specs=pl.BlockSpec(block, lambda k, h, table: (0, k, h, 0))),
        compiler_params=pltpu.CompilerParams(vmem_limit_bytes=VMEM_LIMIT),
        name="place",
    )(table, final, left, right)


def from_behind(value, axis, steps):
    count = lax.axis_size(axis)
    leading, last = (max(0, -steps), min(count, count - steps))
    return lax.ppermute(value, axis, [(source, source + steps) for source in range(leading, last)])


def routes_of(targets, blocks):
    here = lax.axis_index("bxy")
    capacity = blocks // 2
    goal = targets.reshape((blocks,))
    left = from_behind(goal + 1, "bxy", 1) - 1
    right = from_behind(goal + 1, "bxy", -1) - 1
    numbers = jnp.arange(blocks, dtype=jnp.int32)
    ranks = jnp.arange(capacity, dtype=jnp.int32)

    def rank(going):
        return jnp.sum((going[None, :] & (numbers[None, :] < numbers[:, None])).astype(jnp.int32), axis=1)

    def picked(going):
        hit = going[:, None] & (rank(going)[:, None] == ranks[None, :])
        return jnp.sum(jnp.where(hit, numbers[:, None], 0), axis=0)

    def reaching(whose, from_index):
        going = (whose // blocks == here) & (whose >= 0)
        hit = going[:, None] & (whose[:, None] - here * blocks == numbers[None, :])
        return jnp.any(hit, axis=0), jnp.sum(jnp.where(hit, from_index(going)[:, None], 0), axis=0)

    _own, own_index = reaching(goal, lambda going: numbers)
    is_left, left_index = reaching(left, rank)
    is_right, right_index = reaching(right, rank)
    kind = jnp.where(is_left, 1, jnp.where(is_right, 2, 0))
    index = jnp.where(is_left, left_index, jnp.where(is_right, right_index, own_index))
    table = jnp.stack([kind, index], axis=1).astype(jnp.int32)
    return picked(goal // blocks == here + 1), picked(goal // blocks == here - 1), table


def on_device(pdfs, relax, fluid, targets):
    q, blocks, rows, width = pdfs.shape
    edge = rows
    f32 = jnp.float32
    go_right, go_left, table = routes_of(targets, blocks)
    here, row = lax.axis_index("bxy"), lax.axis_index("bz")
    ends = jnp.stack([here == 0, here == lax.axis_size("bxy") - 1, row == 0,
                      row == lax.axis_size("bz") - 1]).astype(jnp.int32)
    full = pl.BlockSpec((q, 1, rows, width), lambda s: (0, s, 0, 0))
    cell = pl.BlockSpec((1, rows, width), lambda s: (s, 0, 0))
    cell_below = pl.BlockSpec((1, rows, width), lambda s: (jnp.maximum(s - 1, 0), 0, 0))
    cell_above = pl.BlockSpec((1, rows, width), lambda s: (jnp.minimum(s + 1, blocks - 1), 0, 0))
    below = pl.BlockSpec((5, 1, rows, width), lambda s: (0, jnp.maximum(s - 1, 0), 0, 0))
    above = pl.BlockSpec((5, 1, rows, width), lambda s: (1, jnp.minimum(s + 1, blocks - 1), 0, 0))
    y_shape, x_shape, c_shape = (2, 6, rows, 128), (2, blocks, 8, width), (4, 8, 128)
    y_spec = pl.BlockSpec(y_shape, lambda s: (0, 0, 0, 0))
    x_all = pl.BlockSpec(x_shape, lambda s: (0, 0, 0, 0))
    x_spec = pl.BlockSpec((2, 1, 8, width), lambda s: (0, s, 0, 0))
    c_spec = pl.BlockSpec(c_shape, lambda s: (0, 0, 0))
    halo_out = [jax.ShapeDtypeStruct(s, f32) for s in (y_shape, x_shape, c_shape)]
    big = jax.ShapeDtypeStruct(pdfs.shape, f32)
    params = pltpu.CompilerParams(vmem_limit_bytes=VMEM_LIMIT)

    post, ys, xs, cs = pl.pallas_call(
        functools.partial(first_kernel, edge), grid=(blocks,),
        out_shape=[big] + halo_out, in_specs=[full, cell, cell],
        out_specs=[full, y_spec, x_spec, c_spec], compiler_params=params, name="first",
    )(pdfs, relax, fluid)
    halo = exchange(ys, xs, cs)
    post, mask, ys, xs, cs = pl.pallas_call(
        functools.partial(middle_kernel, edge), grid=(blocks,),
        out_shape=[big, jax.ShapeDtypeStruct(fluid.shape, jnp.int32)] + halo_out,
        in_specs=[pl.BlockSpec(memory_space=pltpu.SMEM), full, below, above, cell, cell, cell_below, cell_above,
                  y_spec, x_all, c_spec],
        out_specs=[full, cell, y_spec, x_spec, c_spec],
        scratch_shapes=[pltpu.VMEM((q, rows, width), f32)], compiler_params=params, name="middle",
    )(ends, post, post, post, relax, fluid, fluid, fluid, *halo)
    halo = exchange(ys, xs, cs)
    final = pl.pallas_call(
        functools.partial(last_kernel, edge), grid=(blocks,),
        out_shape=big, in_specs=[cell, full, below, above, y_spec, x_all, c_spec],
        out_specs=full, compiler_params=params, name="last",
    )(mask, post, post, post, *halo)
    got_left = from_behind(pack(final, go_right), "bxy", 1)
    got_right = from_behind(pack(final, go_left), "bxy", -1)
    return place(final, got_left, got_right, table)


def solution(mesh):
    placed = (
        P(None, None, "bxy", "bz"),
        P(None, "bxy", "bz"),
        P(None, "bxy", "bz"),
        P("bz", "bxy", None),
    )
    return jax.shard_map(
        on_device, mesh=mesh, in_specs=placed, out_specs=P(None, None, "bxy", "bz"), check_vma=False
    )
```

profile of v0, /device:TPU:1, one launch (start us, length us, event | category | flops | bytes accessed | tf_op | source)
XLA Modules:
  0.0 208.9 jit_solution(2263171432083384966)
XLA Ops:
  0.0 0.7 broadcast_compare_fusion
  0.7 0.7 broadcast_compare_fusion.1
  1.3 0.1 convert_reduce_fusion.1
  1.4 0.6 fusion.9.pick_ref
  2.1 10.9 %first.1 = (f32[19,4,32,1024]{3,2,1,0:T(8,128)}, f32[2,6,32,128]{3,2,1,0:T(8,128)}, f32[2,4,8,1024]{3,2,1,0:T(8,128)}, f32[4,8,128]{2,1,0:T(8,128)}) custom-call(f32[19,4,32,1024]{3,2,1,0:T(8,128)} %pdfs_ref.1, f32[4,32,1024]{2,1,0:T(8,128)} %relax_ref.3, s32[4,32,1024]{2,1,0:T(8,128)} %fabove_ref.1), custom_call_target="tpu_custom_call" | custom-call | tf_op jit(solution)/shard_map/first/pallas_call | solution.py:387
  13.0 0.0 copy-start.3
  13.0 0.9 copy-done.3
  13.9 0.0 copy-start.7
  13.9 0.9 copy-done.7
  14.9 0.0 copy-start.11
  14.9 0.7 copy-done.11
  15.6 11.9 %halo.2 = (f32[2,6,32,128]{3,2,1,0:T(8,128)S(1)}, f32[2,4,8,1024]{3,2,1,0:T(8,128)S(1)}, f32[4,8,128]{2,1,0:T(8,128)S(1)}) custom-call(f32[2,6,32,128]{3,2,1,0:T(8,128)S(1)} %copy-done.7, f32[2,4,8,1024]{3,2,1,0:T(8,128)S(1)} %copy-done.3, f32[4,8,128]{2,1,0:T(8,128)S(1)} %copy-done.11), custom_call_target="tpu_custom_call" | custom-call | tf_op jit(solution)/shard_map/halo/pallas_call | solution.py:143
  27.4 0.0 copy-start
  27.4 0.7 copy-done
  28.1 0.0 copy-start.4
  28.1 0.7 copy-done.4
  28.8 0.0 copy-start.8
  28.8 0.6 copy-done.8
  29.4 0.7 add_convert_fusion.ends_ref
  30.1 19.4 %middle.1 = (f32[19,4,32,1024]{3,2,1,0:T(8,128)}, s32[4,32,1024]{2,1,0:T(8,128)}, f32[2,6,32,128]{3,2,1,0:T(8,128)}, f32[2,4,8,1024]{3,2,1,0:T(8,128)}, f32[4,8,128]{2,1,0:T(8,128)}) custom-call(s32[4]{0:T(128)} %add_convert_fusion.ends_ref, f32[19,4,32,1024]{3,2,1,0:T(8,128)} %get-tuple-element.20.post_ref.below_ref.above_ref, ...), custom_call_target="tpu_custom_call" | custom-call | tf_op jit(solution)/shard_map/middle/pallas_call | solution.py:393
  49.4 0.0 copy-start.2
  49.4 0.9 copy-done.2
  50.4 0.0 copy-start.6
  50.4 0.9 copy-done.6
  51.3 0.0 copy-start.10
  51.3 0.7 copy-done.10
  52.0 10.8 %halo.3 = (f32[2,6,32,128]{3,2,1,0:T(8,128)S(1)}, f32[2,4,8,1024]{3,2,1,0:T(8,128)S(1)}, f32[4,8,128]{2,1,0:T(8,128)S(1)}) custom-call(f32[2,6,32,128]{3,2,1,0:T(8,128)S(1)} %copy-done.6, f32[2,4,8,1024]{3,2,1,0:T(8,128)S(1)} %copy-done.2, f32[4,8,128]{2,1,0:T(8,128)S(1)} %copy-done.10), custom_call_target="tpu_custom_call" | custom-call | tf_op jit(solution)/shard_map/halo/pallas_call | solution.py:143
  62.9 0.0 copy-start.1
  62.9 0.7 copy-done.1
  63.6 0.0 copy-start.5
  63.6 0.7 copy-done.5
  64.3 0.0 copy-start.9
  64.3 0.6 copy-done.9
  64.9 11.5 %last.1.source_ref.final_ref = f32[19,4,32,1024]{3,2,1,0:T(8,128)} custom-call(s32[4,32,1024]{2,1,0:T(8,128)} %get-tuple-element.27.mask_ref, f32[19,4,32,1024]{3,2,1,0:T(8,128)} %get-tuple-element.28.post_ref.below_ref.above_ref, f32[19,4,32,1024]{3,2,1,0:T(8,128)} %get-tuple-element.28.post_ref.below_ref.above_ref, ...), custom_call_target="tpu_custom_call" | custom-call | tf_op jit(solution)/shard_map/last/pallas_call | solution.py:402
  76.4 5.9 %pack.2 = f32[19,2,32,1024]{3,2,1,0:T(8,128)} custom-call(s32[2]{0:T(128)} %fusion.9.pick_ref, f32[19,4,32,1024]{3,2,1,0:T(8,128)} %last.1.source_ref.final_ref), custom_call_target="tpu_custom_call" | custom-call | tf_op jit(solution)/shard_map/pack/pallas_call | solution.py:277
  82.2 0.0 copy-start.12
  82.3 3.1 %collective-permute-start.2 = (f32[19,2,32,1024]{3,2,1,0:T(8,128)}, f32[19,2,32,1024]{3,2,1,0:T(8,128)}, u32[]{:S(2)}, u32[]{:S(2)}) collective-permute-start(f32[19,2,32,1024]{3,2,1,0:T(8,128)} %pack.2), channel_id=1, source_target_pairs={{0,1},{1,2},{2,3},{3,4},{4,5},{5,6},{6,7},{8,9},{9,10},{10,11},{11... | collective-permute-start | bytes 14942216 | tf_op jit(solution)/shard_map/ppermute | solution.py:331
  85.4 0.1 convert_reduce_fusion
  85.5 0.7 fusion.10.pick_ref
  86.2 5.9 %pack.3 = f32[19,2,32,1024]{3,2,1,0:T(8,128)} custom-call(s32[2]{0:T(128)} %fusion.10.pick_ref, f32[19,4,32,1024]{3,2,1,0:T(8,128)} %last.1.source_ref.final_ref), custom_call_target="tpu_custom_call" | custom-call | tf_op jit(solution)/shard_map/pack/pallas_call | solution.py:277
  92.1 3.6 %collective-permute-start.3 = (f32[19,2,32,1024]{3,2,1,0:T(8,128)}, f32[19,2,32,1024]{3,2,1,0:T(8,128)}, u32[]{:S(2)}, u32[]{:S(2)}) collective-permute-start(f32[19,2,32,1024]{3,2,1,0:T(8,128)} %pack.3), channel_id=1, source_target_pairs={{1,0},{2,1},{3,2},{4,3},{5,4},{6,5},{7,6},{9,8},{10,9},{11,10},{12... | collective-permute-start | bytes 14942216 | tf_op jit(solution)/shard_map/ppermute | solution.py:331
  95.7 0.0 copy-done.12
  95.7 1.9 collective-permute-start.1
  97.6 3.6 %collective-permute-start = (s32[4]{0:T(128)S(1)}, s32[4]{0:T(128)S(1)}, u32[]{:S(2)}, u32[]{:S(2)}) collective-permute-start(s32[4]{0:T(128)S(1)} %get-tuple-element.42), channel_id=1, source_target_pairs={{0,1},{1,2},{2,3},{3,4},{4,5},{5,6},{6,7},{8,9},{9,10},{10,11},{11... | collective-permute-start | bytes 56 | tf_op jit(solution)/shard_map/ppermute | solution.py:331
  101.3 0.1 select_reduce_fusion
  101.4 93.9 %collective-permute-done.1 = s32[4]{0:T(128)S(1)} collective-permute-done((s32[4]{0:T(128)S(1)}, s32[4]{0:T(128)S(1)}, u32[]{:S(2)}, u32[]{:S(2)}) %collective-permute-start.1) | collective-permute-done | bytes 48 | tf_op jit(solution)/shard_map/ppermute | solution.py:331
  195.3 0.1 convert_reduce_fusion.2
  195.5 0.0 collective-permute-done
  195.5 0.1 convert_reduce_fusion.3
  195.6 0.1 fusion.7
  195.7 0.1 fusion.8
  195.8 0.1 select_reduce_fusion.1
  195.9 0.1 select_reduce_fusion.2
  196.0 0.1 copy.7
  196.1 0.1 copy.8
  196.2 0.7 pad_add_fusion.table_ref
  196.8 0.0 collective-permute-done.2.left_ref
  196.8 0.0 collective-permute-done.3.right_ref
  196.8 12.1 %place.1 = f32[19,4,32,1024]{3,2,1,0:T(8,128)} custom-call(s32[4,2]{1,0:T(4,128)} %pad_add_fusion.table_ref, f32[19,4,32,1024]{3,2,1,0:T(8,128)} %last.1.source_ref.final_ref, f32[19,2,32,1024]{3,2,1,0:T(8,128)} %collective-permute-done.2.left_ref, f32[19,2,32,1024]{3,2,1,0:T(8,128)} %collective-permute-done.3.right_ref), custom_call_target="tpu_custom_call" | custom-call | tf_op jit(solution)/shard_map/place/pallas_call | solution.py:316
  (6 shorter events, 0.0 us)
Async XLA Ops:
  13.0 1.0 copy-start.3
  13.9 0.9 copy-start.7
  14.9 0.7 copy-start.11
  27.4 0.7 copy-start
  28.1 0.7 copy-start.4
  28.8 0.6 copy-start.8
  49.4 1.0 copy-start.2
  50.4 0.9 copy-start.6
  51.3 0.7 copy-start.10
  62.9 0.7 copy-start.1
  63.6 0.7 copy-start.5
  64.3 0.6 copy-start.9
  82.2 13.4 %copy-start.12 = (s32[1,1,4]{2,1,0:T(1,128)S(1)}, s32[1,1,4]{2,1,0:T(1,128)}, u32[]{:S(2)}) copy-start(s32[1,1,4]{2,1,0:T(1,128)} %param.7) | copy-start | bytes 52
  82.3 114.6 %collective-permute-start.2 = (f32[19,2,32,1024]{3,2,1,0:T(8,128)}, f32[19,2,32,1024]{3,2,1,0:T(8,128)}, u32[]{:S(2)}, u32[]{:S(2)}) collective-permute-start(f32[19,2,32,1024]{3,2,1,0:T(8,128)} %pack.2), channel_id=1, source_target_pairs={{0,1},{1,2},{2,3},{3,4},{4,5},{5,6},{6,7},{8,9},{9,10},{10,11},{11... | collective-permute-start | bytes 14942216 | tf_op jit(solution)/shard_map/ppermute | solution.py:331
  92.1 104.8 %collective-permute-start.3 = (f32[19,2,32,1024]{3,2,1,0:T(8,128)}, f32[19,2,32,1024]{3,2,1,0:T(8,128)}, u32[]{:S(2)}, u32[]{:S(2)}) collective-permute-start(f32[19,2,32,1024]{3,2,1,0:T(8,128)} %pack.3), channel_id=1, source_target_pairs={{1,0},{2,1},{3,2},{4,3},{5,4},{6,5},{7,6},{9,8},{10,9},{11,10},{12... | collective-permute-start | bytes 14942216 | tf_op jit(solution)/shard_map/ppermute | solution.py:331
  95.7 99.6 %collective-permute-start.1 = (s32[4]{0:T(128)S(1)}, s32[4]{0:T(128)S(1)}, u32[]{:S(2)}, u32[]{:S(2)}) collective-permute-start(s32[4]{0:T(128)S(1)} %get-tuple-element.42), channel_id=1, source_target_pairs={{1,0},{2,1},{3,2},{4,3},{5,4},{6,5},{7,6},{9,8},{10,9},{11,10},{12... | collective-permute-start | bytes 56 | tf_op jit(solution)/shard_map/ppermute | solution.py:331
  97.6 97.8 %collective-permute-start = (s32[4]{0:T(128)S(1)}, s32[4]{0:T(128)S(1)}, u32[]{:S(2)}, u32[]{:S(2)}) collective-permute-start(s32[4]{0:T(128)S(1)} %get-tuple-element.42), channel_id=1, source_target_pairs={{0,1},{1,2},{2,3},{3,4},{4,5},{5,6},{6,7},{8,9},{9,10},{10,11},{11... | collective-permute-start | bytes 56 | tf_op jit(solution)/shard_map/ppermute | solution.py:331
where the time goes:
time: 210 us; the launch traced here: 209 us
  waiting for transfers between devices  93.9 us (45%)
  Pallas kernels  88.3 us (42%)
  starting transfers between devices  12.3 us (6%)
  local copies, waits for them, and re-layouts  9.29 us (4%)
  other arithmetic  4.98 us (2%)
    ppermute x4, waiting for transfers between devices, from_behind(): lax.ppermute(value, axis, [(source, source + steps) for source in range(l...  93.9 us
    pallas_call x2, Pallas kernels, exchange(): pl.pallas_call(halo_kernel, out_shape=[jax.ShapeDtypeStruct(a.shape, a.dt...  22.7 us
    pallas_call x1, Pallas kernels, on_device(): pl.pallas_call(functools.partial(middle_kernel, edge), grid=(blocks,), ou...  19.4 us
    ppermute x4, starting transfers between devices, from_behind(): lax.ppermute(value, axis, [(source, source + steps) for source in range(l...  12.3 us
    pallas_call x1, Pallas kernels, place(): pl.pallas_call(place_kernel, out_shape=jax.ShapeDtypeStruct(final.shape,...  12.1 us
    pallas_call x2, Pallas kernels, pack(): pl.pallas_call(pack_kernel, out_shape=jax.ShapeDtypeStruct((q, count, row...  11.7 us
    pallas_call x1, Pallas kernels, on_device(): pl.pallas_call(functools.partial(last_kernel, edge), grid=(blocks,), out_...  11.5 us
    pallas_call x1, Pallas kernels, on_device(): pl.pallas_call(functools.partial(first_kernel, edge), grid=(blocks,), out...  10.9 us
  transfers between devices with their start and end apart: 4, of which 1 were waited for; matrix products, arithmetic and copies ran while one was open for 1% of the time, Pallas kernels for 3%

commit v1 on v0

--- a/solution.py
+++ b/solution.py
@@ -1,4 +1,5 @@
 import functools
+import math
 
 import jax
 import jax.numpy as jnp
@@ -112,30 +113,50 @@
     emit_halo(slot, slot == pl.num_programs(0) - 1, edge, post_ref, fluid_ref, ys_ref, xs_ref, cs_ref)
 
 
+def remote(src, dst, send_sem, recv_sem, device):
+    return pltpu.make_async_remote_copy(
+        src_ref=src, dst_ref=dst, send_sem=send_sem, recv_sem=recv_sem, device_id=device, device_id_type=MESH)
+
+
 def halo_kernel(ys, xs, cs, yr, xr, cr, send_sem, recv_sem):
     nz, nb = lax.axis_size("bz"), lax.axis_size("bxy")
     z, b = lax.axis_index("bz"), lax.axis_index("bxy")
 
-    def device(dz, db):
-        return (lax.rem(z + dz + nz, nz), lax.rem(b + db + nb, nb))
+    def there(dz, db):
+        exists = None
+        for at, step, count in ((z, dz, nz), (b, db, nb)):
+            if step:
+                inside = at < count - 1 if step == 1 else at > 0
+                exists = inside if exists is None else exists & inside
+        return exists
 
     routes = [(ys.at[0], yr.at[0], 1, 0), (ys.at[1], yr.at[1], -1, 0),
               (xs.at[0], xr.at[0], 0, 1), (xs.at[1], xr.at[1], 0, -1)]
     for k, i in enumerate(CORNERS):
         routes.append((cs.at[k], cr.at[k], VELOCITIES[i][1], VELOCITIES[i][0]))
     barrier = pltpu.get_barrier_semaphore()
+    count = 0
     for _s, _d, dz, db in routes:
-        pl.semaphore_signal(barrier, inc=1, device_id=device(dz, db), device_id_type=MESH)
-    pl.semaphore_wait(barrier, len(routes))
-    copies = []
+        count = count + there(dz, db).astype(jnp.int32)
+
+        @pl.when(there(dz, db))
+        def _():
+            pl.semaphore_signal(barrier, inc=1, device_id=(z + dz, b + db), device_id_type=MESH)
+
+    pl.semaphore_wait(barrier, count)
     for n, (src, dst, dz, db) in enumerate(routes):
-        copy = pltpu.make_async_remote_copy(
-            src_ref=src, dst_ref=dst, send_sem=send_sem.at[n], recv_sem=recv_sem.at[n],
-            device_id=device(dz, db), device_id_type=MESH)
-        copy.start()
-        copies.append(copy)
-    for copy in copies:
-        copy.wait()
+        @pl.when(there(dz, db))
+        def _():
+            remote(src, dst, send_sem.at[n], recv_sem.at[n], (z + dz, b + db)).start()
+
+    for n, (src, dst, dz, db) in enumerate(routes):
+        @pl.when(there(dz, db))
+        def _():
+            remote(src, dst, send_sem.at[n], recv_sem.at[n], (z + dz, b + db)).wait_send()
+
+        @pl.when(there(-dz, -db))
+        def _():
+            remote(src, dst, send_sem.at[n], recv_sem.at[n], (z - dz, b - db)).wait_recv()
 
 
 def exchange(ys, xs, cs):
@@ -257,37 +278,117 @@
     emit_halo(slot, slot == slots - 1, edge, out_ref, fluid_ref, ys_ref, xs_ref, cs_ref)
 
 
-def last_kernel(edge, mask_ref, post_ref, below_ref, above_ref, yr_ref, xr_ref, cr_ref, out_ref):
+def last_kernel(edge, plan_ref, mask_ref, post_ref, below_ref, above_ref, yr_ref, xr_ref, cr_ref,
+                right_ref, left_ref, kept_ref, next_ref):
     def write(i, value):
-        out_ref[i, 0] = value
-
-    stream_block(pl.program_id(0), edge, pl.num_programs(0), mask_ref, post_ref, below_ref, above_ref,
+        next_ref[i, 0] = value
+
+    g = pl.program_id(0)
+    stream_block(plan_ref[0, g], edge, pl.num_programs(0), mask_ref, post_ref, below_ref, above_ref,
                  yr_ref, xr_ref, cr_ref, write)
-
-
-def pack_kernel(pick_ref, source_ref, out_ref):
-    out_ref[...] = source_ref[...]
-
-
-def pack(final, pick):
-    q, _blocks, rows, width = final.shape
-    count = pick.shape[0]
-    parts = 2 if rows % 16 == 0 else 1
-    block = (q, 1, rows // parts, width)
-    return pl.pallas_call(
-        pack_kernel,
-        out_shape=jax.ShapeDtypeStruct((q, count, rows, width), final.dtype),
-        grid_spec=pltpu.PrefetchScalarGridSpec(
-            num_scalar_prefetch=1, grid=(count, parts),
-            in_specs=[pl.BlockSpec(block, lambda g, h, pick: (0, pick[g], h, 0))],
-            out_specs=pl.BlockSpec(block, lambda g, h, pick: (0, g, h, 0))),
-        compiler_params=pltpu.CompilerParams(vmem_limit_bytes=VMEM_LIMIT),
-        name="pack",
-    )(pick, final)
+    for kind, out_ref in enumerate((right_ref, left_ref, kept_ref)):
+        @pl.when(plan_ref[1, g] == kind)
+        def _():
+            def copy(i, carry):
+                out_ref[i] = next_ref[i]
+                return carry
+
+            lax.fori_loop(0, Q, copy, 0)
+
+
+def migrate_kernel(right, left, from_left, from_right, passing, send_sem, recv_sem):
+    nb = lax.axis_size("bxy")
+    z, b = lax.axis_index("bz"), lax.axis_index("bxy")
+    half = (Q + 1) // 2
+    cuts = (0, half // 2, half, half + (Q - half + 1) // 2, Q)
+    chunks = [(n, slice(cuts[n], cuts[n + 1]), n < 2) for n in range(4)]
+    across = math.isqrt(nb // 2)
+    row = 2 * across
+    bends = across == 2 and nb == 2 * row
+    cut = row - 1 if bends else nb
+    low, high = cut + 1 - row, cut + row
+    no = b < 0
+    goes_right, goes_left = (b < nb - 1) & (b != cut), (b > 0) & (b != cut + 1)
+    at_cut, past_cut, is_low, is_high = (
+        (b == cut, b == cut + 1, b == low, b == high) if bends else (no, no, no, no))
+    meets = [(goes_right, b + 1), (goes_left, b - 1)]
+    if bends:
+        for who in (at_cut, past_cut):
+            meets += [(who, low), (who, high)]
+        for who in (is_low, is_high):
+            meets += [(who, cut), (who, cut + 1)]
+    barrier = pltpu.get_barrier_semaphore()
+    count = 0
+    for who, peer in meets:
+        count = count + who.astype(jnp.int32)
+
+        @pl.when(who)
+        def _():
+            pl.semaphore_signal(barrier, inc=1, device_id=(z, peer), device_id_type=MESH)
+
+    pl.semaphore_wait(barrier, count)
+
+    def copy(src, dst, c, part, sent, got, peer):
+        return remote(src.at[part], dst.at[part], send_sem.at[sent, c], recv_sem.at[got, c], (z, peer))
+
+    for c, part, first in chunks:
+        @pl.when(goes_right)
+        def _():
+            copy(right, from_left, c, part, 0, 0, b + 1).start()
+
+        @pl.when(goes_left)
+        def _():
+            copy(left, from_right, c, part, 1, 1, b - 1).start()
+
+        if bends:
+            @pl.when(at_cut)
+            def _():
+                copy(right, passing, c, part, 0, 2, low if first else high).start()
+
+            @pl.when(past_cut)
+            def _():
+                copy(left, passing, c, part, 1, 2, high if first else low).start()
+
+    if bends:
+        for who, ahead in ((is_low, True), (is_high, False)):
+            @pl.when(who)
+            def _():
+                for n in (0, 2, 1, 3):
+                    c, part, first = chunks[n]
+                    copy(right, passing, c, part, 2, 2, cut).wait_recv()
+                    if first == ahead:
+                        copy(passing, from_left, c, part, 2, 0, cut + 1).start()
+                    else:
+                        copy(passing, from_right, c, part, 2, 1, cut).start()
+                for c, part, first in chunks:
+                    copy(passing, from_left, c, part, 2, 0, cut).wait_send()
+
+    for c, part, first in chunks:
+        @pl.when(b < nb - 1)
+        def _():
+            copy(right, from_left, c, part, 0, 0, b + 1).wait_send()
+            copy(left, from_right, c, part, 1, 1, b + 1).wait_recv()
+
+        @pl.when(b > 0)
+        def _():
+            copy(left, from_right, c, part, 1, 1, b - 1).wait_send()
+            copy(right, from_left, c, part, 0, 0, b - 1).wait_recv()
+
+
+def migrate(right, left):
+    hbm = pl.BlockSpec(memory_space=pl.ANY)
+    shape = jax.ShapeDtypeStruct(right.shape, right.dtype)
+    from_left, from_right, _passing = pl.pallas_call(
+        migrate_kernel, out_shape=[shape] * 3, in_specs=[hbm] * 2, out_specs=[hbm] * 3,
+        scratch_shapes=[pltpu.SemaphoreType.DMA((3, 4)), pltpu.SemaphoreType.DMA((3, 4))],
+        compiler_params=pltpu.CompilerParams(collective_id=1, has_side_effects=True, vmem_limit_bytes=VMEM_LIMIT),
+        name="migrate",
+    )(right, left)
+    return from_left, from_right
 
 
 def place_kernel(table_ref, final_ref, left_ref, right_ref, out_ref):
-    kind = table_ref[pl.program_id(0), 0]
+    kind = table_ref[3, pl.program_id(0)]
 
     @pl.when(kind == 0)
     def _():
@@ -304,22 +405,18 @@
 
 def place(final, left, right, table):
     q, blocks, rows, width = final.shape
-    parts = 2 if rows % 16 == 0 else 1
-    block = (q, 1, rows // parts, width)
+    block = (q, 1, rows, width)
 
     def taken(kind):
-        def index(k, h, table):
-            used = table[k, 0] == kind
-            return (0, jnp.where(used, table[k, 1], 0), jnp.where(used, h, 0), 0)
-        return pl.BlockSpec(block, index)
+        return pl.BlockSpec(block, lambda k, table: (0, table[kind, k], 0, 0))
 
     return pl.pallas_call(
         place_kernel,
         out_shape=jax.ShapeDtypeStruct(final.shape, final.dtype),
         grid_spec=pltpu.PrefetchScalarGridSpec(
-            num_scalar_prefetch=1, grid=(blocks, parts),
+            num_scalar_prefetch=1, grid=(blocks,),
             in_specs=[taken(0), taken(1), taken(2)],
-            out_specs=pl.BlockSpec(block, lambda k, h, table: (0, k, h, 0))),
+            out_specs=pl.BlockSpec(block, lambda k, table: (0, k, 0, 0))),
         compiler_params=pltpu.CompilerParams(vmem_limit_bytes=VMEM_LIMIT),
         name="place",
     )(table, final, left, right)
@@ -333,39 +430,53 @@
 
 def routes_of(targets, blocks):
     here = lax.axis_index("bxy")
-    capacity = blocks // 2
     goal = targets.reshape((blocks,))
     left = from_behind(goal + 1, "bxy", 1) - 1
     right = from_behind(goal + 1, "bxy", -1) - 1
     numbers = jnp.arange(blocks, dtype=jnp.int32)
-    ranks = jnp.arange(capacity, dtype=jnp.int32)
 
     def rank(going):
         return jnp.sum((going[None, :] & (numbers[None, :] < numbers[:, None])).astype(jnp.int32), axis=1)
-
-    def picked(going):
-        hit = going[:, None] & (rank(going)[:, None] == ranks[None, :])
-        return jnp.sum(jnp.where(hit, numbers[:, None], 0), axis=0)
 
     def reaching(whose, from_index):
         going = (whose // blocks == here) & (whose >= 0)
         hit = going[:, None] & (whose[:, None] - here * blocks == numbers[None, :])
         return jnp.any(hit, axis=0), jnp.sum(jnp.where(hit, from_index(going)[:, None], 0), axis=0)
 
-    _own, own_index = reaching(goal, lambda going: numbers)
     is_left, left_index = reaching(left, rank)
     is_right, right_index = reaching(right, rank)
     kind = jnp.where(is_left, 1, jnp.where(is_right, 2, 0))
-    index = jnp.where(is_left, left_index, jnp.where(is_right, right_index, own_index))
-    table = jnp.stack([kind, index], axis=1).astype(jnp.int32)
-    return picked(goal // blocks == here + 1), picked(goal // blocks == here - 1), table
+    index = jnp.where(is_left, left_index, jnp.where(is_right, right_index, numbers))
+    used = kind[None, :, None] == jnp.arange(3, dtype=jnp.int32)[:, None, None]
+    before = used & (numbers[:, None] <= numbers[None, :])[None]
+    latest = jnp.max(jnp.where(before, numbers[None, :, None], -1), axis=1)
+    held = jnp.sum(jnp.where(numbers[None, :, None] == latest[:, None, :], index[None, :, None], 0), axis=1)
+    table = jnp.concatenate([held, kind[None]], axis=0).astype(jnp.int32)
+
+    way = jnp.where(goal // blocks == here + 1, 0, jnp.where(goal // blocks == here - 1, 1, 2))
+    key = way * blocks + numbers
+    place_of = jnp.sum((key[None, :] < key[:, None]).astype(jnp.int32), axis=1)
+    rights = jnp.sum((way == 0).astype(jnp.int32))
+    lefts = jnp.sum((way == 1).astype(jnp.int32))
+
+    def in_order(values, positions):
+        return jnp.sum(jnp.where(place_of[:, None] == positions[None, :], values[:, None], 0), axis=0)
+
+    stays = jnp.minimum(jnp.maximum(numbers, rights + lefts), blocks - 1)
+    plan = jnp.stack([
+        in_order(numbers, numbers), in_order(way, numbers),
+        jnp.minimum(numbers, jnp.maximum(rights - 1, 0)),
+        jnp.maximum(jnp.minimum(numbers - rights, lefts - 1), 0),
+        in_order(goal % blocks, stays),
+    ]).astype(jnp.int32)
+    return plan, table
 
 
 def on_device(pdfs, relax, fluid, targets):
     q, blocks, rows, width = pdfs.shape
     edge = rows
     f32 = jnp.float32
-    go_right, go_left, table = routes_of(targets, blocks)
+    plan, table = routes_of(targets, blocks)
     here, row = lax.axis_index("bxy"), lax.axis_index("bz")
     ends = jnp.stack([here == 0, here == lax.axis_size("bxy") - 1, row == 0,
                       row == lax.axis_size("bz") - 1]).astype(jnp.int32)
@@ -399,14 +510,33 @@
         scratch_shapes=[pltpu.VMEM((q, rows, width), f32)], compiler_params=params, name="middle",
     )(ends, post, post, post, relax, fluid, fluid, fluid, *halo)
     halo = exchange(ys, xs, cs)
-    final = pl.pallas_call(
-        functools.partial(last_kernel, edge), grid=(blocks,),
-        out_shape=big, in_specs=[cell, full, below, above, y_spec, x_all, c_spec],
-        out_specs=full, compiler_params=params, name="last",
-    )(mask, post, post, post, *halo)
-    got_left = from_behind(pack(final, go_right), "bxy", 1)
-    got_right = from_behind(pack(final, go_left), "bxy", -1)
-    return place(final, got_left, got_right, table)
+    def moved(spec, shift):
+        shape = spec.block_shape
+        if len(shape) == 3:
+            return pl.BlockSpec(shape, lambda g, plan: (plan[0, g], 0, 0))
+        lead = 1 if shift == 1 else 0
+        return pl.BlockSpec(
+            shape, lambda g, plan: (lead, jnp.minimum(jnp.maximum(plan[0, g] + shift, 0), blocks - 1), 0, 0))
+
+    def whole(shape):
+        return pl.BlockSpec(shape, lambda g, plan: (0,) * len(shape))
+
+    def out(row):
+        return pl.BlockSpec((q, 1, rows, width), lambda g, plan: (0, plan[row, g], 0, 0))
+
+    sent = jax.ShapeDtypeStruct((q, blocks // 2, rows, width), f32)
+    right, left, kept = pl.pallas_call(
+        functools.partial(last_kernel, edge), out_shape=[sent, sent, big],
+        grid_spec=pltpu.PrefetchScalarGridSpec(
+            num_scalar_prefetch=1, grid=(blocks,),
+            in_specs=[moved(cell, 0), moved(full, 0), moved(below, -1), moved(above, 1),
+                      whole(y_shape), whole(x_shape), whole(c_shape)],
+            out_specs=[out(2), out(3), out(4)],
+            scratch_shapes=[pltpu.VMEM((q, 1, rows, width), f32)]),
+        compiler_params=params, name="last",
+    )(plan, mask, post, post, post, *halo)
+    from_left, from_right = migrate(right, left)
+    return place(kept, from_left, from_right, table)
 
 
 def solution(mesh):

time: 210 us -> 177 us (0.84)
  waiting for transfers between devices: 93.9 us -> 0.01 us
  Pallas kernels: 88.3 us -> 153 us
  starting transfers between devices: 12.3 us -> 6.42 us
  between operations: 0.15 us -> 2.86 us
    ppermute x4 -> x2, waiting for transfers between devices: 93.9 us -> 0.01 us  [from_behind(): lax.ppermute(value, axis, [(source, source + steps) for source in range(l...]
    pallas_call x3 -> x2, Pallas kernels: 23.3 us -> 97.4 us  [the longest x1 83.8 us: migrate(): pl.pallas_call(migrate_kernel, out_shape=[shape] * 3, in_specs=[hbm] * 2,...]
    pallas_call x2, Pallas kernels: 22.7 us -> 15.1 us  [exchange(): pl.pallas_call(halo_kernel, out_shape=[jax.ShapeDtypeStruct(a.shape, a.dt...]
    ppermute x4 -> x2, starting transfers between devices: 12.3 us -> 6.42 us  [from_behind(): lax.ppermute(value, axis, [(source, source + steps) for source in range(l...]
    pallas_call x1, Pallas kernels: 12.1 us -> 9.93 us  [place(): pl.pallas_call(place_kernel, out_shape=jax.ShapeDtypeStruct(final.shape,...]
    unnamed x26 -> x24, local copies, waits for them, and re-layouts: 9.1 us -> 9.13 us
  transfers between devices with their start and end apart: 4 -> 2, of which waited for: 1 -> 0; matrix products, arithmetic and copies ran while one was open for 1% -> 2% of each run, Pallas kernels for 3% -> 81%
where the time goes in v1:
time: 177 us; the launch traced here: 176 us
  Pallas kernels  153 us (86%)
  local copies, waits for them, and re-layouts  9.74 us (6%)
  starting transfers between devices  6.42 us (4%)
  other arithmetic  4.44 us (3%)
  between operations  2.86 us (2%)
    pallas_call x1, Pallas kernels, migrate(): pl.pallas_call(migrate_kernel, out_shape=[shape] * 3, in_specs=[hbm] * 2,...  83.8 us
    pallas_call x1, Pallas kernels, on_device(): pl.pallas_call(functools.partial(middle_kernel, edge), grid=(blocks,), ou...  19.4 us
    pallas_call x2, Pallas kernels, exchange(): pl.pallas_call(halo_kernel, out_shape=[jax.ShapeDtypeStruct(a.shape, a.dt...  15.1 us
    pallas_call x1, Pallas kernels, on_device(): pl.pallas_call(functools.partial(last_kernel, edge), out_shape=[sent, sen...  13.6 us
    pallas_call x1, Pallas kernels, on_device(): pl.pallas_call(functools.partial(first_kernel, edge), grid=(blocks,), out...  10.9 us
    pallas_call x1, Pallas kernels, place(): pl.pallas_call(place_kernel, out_shape=jax.ShapeDtypeStruct(final.shape,...  9.93 us
    unnamed x24, local copies, waits for them, and re-layouts  9.13 us
    ppermute x2, starting transfers between devices, from_behind(): lax.ppermute(value, axis, [(source, source + steps) for source in range(l...  6.42 us
  transfers between devices with their start and end apart: 2, of which 0 were waited for; matrix products, arithmetic and copies ran while one was open for 2% of the time, Pallas kernels for 81%

profile of v1, /device:TPU:1, one launch (start us, length us, event | category | flops | bytes accessed | tf_op | source)
XLA Modules:
  0.0 176.1 jit_solution(18286831059050429465)
XLA Ops:
  0.0 0.7 iota_add_fusion
  0.7 1.9 %collective-permute-start.1 = (s32[4]{0:T(128)S(1)}, s32[4]{0:T(128)S(1)}, u32[]{:S(2)}, u32[]{:S(2)}) collective-permute-start(s32[4]{0:T(128)S(1)} %get-tuple-element.55), channel_id=1, source_target_pairs={{1,0},{2,1},{3,2},{4,3},{5,4},{6,5},{7,6},{9,8},{10,9},{11,10},{12... | collective-permute-start | bytes 56 | tf_op jit(solution)/shard_map/ppermute | solution.py:428
  2.6 4.5 %collective-permute-start = (s32[4]{0:T(128)S(1)}, s32[4]{0:T(128)S(1)}, u32[]{:S(2)}, u32[]{:S(2)}) collective-permute-start(s32[4]{0:T(128)S(1)} %get-tuple-element.55), channel_id=1, source_target_pairs={{0,1},{1,2},{2,3},{3,4},{4,5},{5,6},{6,7},{8,9},{9,10},{10,11},{11... | collective-permute-start | bytes 56 | tf_op jit(solution)/shard_map/ppermute | solution.py:428
  7.1 0.7 fusion.7
  10.5 0.2 convert_reduce_fusion
  10.7 0.7 minimum_maximum_fusion
  11.4 10.9 %first.1 = (f32[19,4,32,1024]{3,2,1,0:T(8,128)}, f32[2,6,32,128]{3,2,1,0:T(8,128)}, f32[2,4,8,1024]{3,2,1,0:T(8,128)}, f32[4,8,128]{2,1,0:T(8,128)}) custom-call(f32[19,4,32,1024]{3,2,1,0:T(8,128)} %pdfs_ref.1, f32[4,32,1024]{2,1,0:T(8,128)} %relax_ref.3, s32[4,32,1024]{2,1,0:T(8,128)} %fabove_ref.1), custom_call_target="tpu_custom_call" | custom-call | tf_op jit(solution)/shard_map/first/pallas_call | solution.py:498
  22.3 0.0 copy-start.3
  22.4 0.9 copy-done.3
  23.3 0.0 copy-start.7
  23.3 0.9 copy-done.7
  24.2 0.0 copy-start.11
  24.2 0.7 copy-done.11
  24.9 7.7 %halo.2 = (f32[2,6,32,128]{3,2,1,0:T(8,128)S(1)}, f32[2,4,8,1024]{3,2,1,0:T(8,128)S(1)}, f32[4,8,128]{2,1,0:T(8,128)S(1)}) custom-call(f32[2,6,32,128]{3,2,1,0:T(8,128)S(1)} %copy-done.7, f32[2,4,8,1024]{3,2,1,0:T(8,128)S(1)} %copy-done.3, f32[4,8,128]{2,1,0:T(8,128)S(1)} %copy-done.11), custom_call_target="tpu_custom_call" | custom-call | tf_op jit(solution)/shard_map/halo/pallas_call | solution.py:164
  32.7 0.0 copy-start.1
  32.7 0.7 copy-done.1
  33.4 0.0 copy-start.5
  33.4 0.7 copy-done.5
  34.1 0.0 copy-start.9
  34.1 0.6 copy-done.9
  34.7 0.7 add_convert_fusion.ends_ref
  35.3 19.4 %middle.1 = (f32[19,4,32,1024]{3,2,1,0:T(8,128)}, s32[4,32,1024]{2,1,0:T(8,128)}, f32[2,6,32,128]{3,2,1,0:T(8,128)}, f32[2,4,8,1024]{3,2,1,0:T(8,128)}, f32[4,8,128]{2,1,0:T(8,128)}) custom-call(s32[4]{0:T(128)} %add_convert_fusion.ends_ref, f32[19,4,32,1024]{3,2,1,0:T(8,128)} %get-tuple-element.25.post_ref.below_ref.above_ref, ...), custom_call_target="tpu_custom_call" | custom-call | tf_op jit(solution)/shard_map/middle/pallas_call | solution.py:504
  54.7 0.0 copy-start.2
  54.7 0.9 copy-done.2
  55.7 0.0 copy-start.6
  55.7 0.9 copy-done.6
  56.6 0.0 copy-start.10
  56.6 0.7 copy-done.10
  57.3 7.4 %halo.3 = (f32[2,6,32,128]{3,2,1,0:T(8,128)S(1)}, f32[2,4,8,1024]{3,2,1,0:T(8,128)S(1)}, f32[4,8,128]{2,1,0:T(8,128)S(1)}) custom-call(f32[2,6,32,128]{3,2,1,0:T(8,128)S(1)} %copy-done.6, f32[2,4,8,1024]{3,2,1,0:T(8,128)S(1)} %copy-done.2, f32[4,8,128]{2,1,0:T(8,128)S(1)} %copy-done.10), custom_call_target="tpu_custom_call" | custom-call | tf_op jit(solution)/shard_map/halo/pallas_call | solution.py:164
  64.7 0.0 copy-start
  64.7 0.7 copy-done
  65.4 0.0 copy-start.4
  65.4 0.7 copy-done.4
  66.1 0.0 copy-start.8
  66.1 0.6 copy-done.8
  66.7 0.1 select_reduce_fusion.2
  66.8 0.6 stack.32.plan_ref
  67.4 13.6 %last.1 = (f32[19,2,32,1024]{3,2,1,0:T(8,128)}, f32[19,2,32,1024]{3,2,1,0:T(8,128)}, f32[19,4,32,1024]{3,2,1,0:T(8,128)}) custom-call(s32[5,4]{1,0:T(8,128)} %stack.32.plan_ref, s32[4,32,1024]{2,1,0:T(8,128)} %get-tuple-element.32.mask_ref, f32[19,4,32,1024]{3,2,1,0:T(8,128)} %get-tuple-element.33.post_ref.below_ref.above_ref, ...), custom_call_target="tpu_custom_call" | custom-call | tf_op jit(solution)/shard_map/last/pallas_call | solution.py:528
  81.0 83.8 %migrate.1 = (f32[19,2,32,1024]{3,2,1,0:T(8,128)}, f32[19,2,32,1024]{3,2,1,0:T(8,128)}, f32[19,2,32,1024]{3,2,1,0:T(8,128)}) custom-call(f32[19,2,32,1024]{3,2,1,0:T(8,128)} %get-tuple-element.41.right, f32[19,2,32,1024]{3,2,1,0:T(8,128)} %get-tuple-element.42.left), custom_call_target="tpu_custom_call" | custom-call | tf_op jit(solution)/shard_map/migrate/pallas_call | solution.py:381
  164.7 0.0 collective-permute-done.1
  164.8 0.1 convert_reduce_fusion.1
  164.9 0.1 fusion.4
  165.0 0.1 select_reduce_fusion.5
  165.1 0.0 collective-permute-done
  165.1 0.1 convert_reduce_fusion.2
  165.2 0.1 fusion.5
  165.3 0.1 select_reduce_fusion.6
  165.4 0.1 select_reduce_fusion.1
  165.5 0.1 select_reduce_fusion
  165.6 0.6 pad_add_fusion.table_ref
  166.2 9.9 %place.1 = f32[19,4,32,1024]{3,2,1,0:T(8,128)} custom-call(s32[4,4]{1,0:T(4,128)} %pad_add_fusion.table_ref, f32[19,4,32,1024]{3,2,1,0:T(8,128)} %get-tuple-element.40.final_ref, f32[19,2,32,1024]{3,2,1,0:T(8,128)} %get-tuple-element.43.left_ref, f32[19,2,32,1024]{3,2,1,0:T(8,128)} %get-tuple-element.44.right_ref), custom_call_target="tpu_custom_call" | custom-call | tf_op jit(solution)/shard_map/place/pallas_call | solution.py:413
  (9 shorter events, 0.1 us)
Async XLA Ops:
  0.7 164.1 %collective-permute-start.1 = (s32[4]{0:T(128)S(1)}, s32[4]{0:T(128)S(1)}, u32[]{:S(2)}, u32[]{:S(2)}) collective-permute-start(s32[4]{0:T(128)S(1)} %get-tuple-element.55), channel_id=1, source_target_pairs={{1,0},{2,1},{3,2},{4,3},{5,4},{6,5},{7,6},{9,8},{10,9},{11,10},{12... | collective-permute-start | bytes 56 | tf_op jit(solution)/shard_map/ppermute | solution.py:428
  2.6 162.5 %collective-permute-start = (s32[4]{0:T(128)S(1)}, s32[4]{0:T(128)S(1)}, u32[]{:S(2)}, u32[]{:S(2)}) collective-permute-start(s32[4]{0:T(128)S(1)} %get-tuple-element.55), channel_id=1, source_target_pairs={{0,1},{1,2},{2,3},{3,4},{4,5},{5,6},{6,7},{8,9},{9,10},{10,11},{11... | collective-permute-start | bytes 56 | tf_op jit(solution)/shard_map/ppermute | solution.py:428
  22.3 1.0 copy-start.3
  23.3 0.9 copy-start.7
  24.2 0.7 copy-start.11
  32.7 0.7 copy-start.1
  33.4 0.7 copy-start.5
  34.1 0.6 copy-start.9
  54.7 1.0 copy-start.2
  55.7 0.9 copy-start.6
  56.6 0.7 copy-start.10
  64.7 0.7 copy-start
  65.4 0.7 copy-start.4
  66.1 0.6 copy-start.8

commit v2 on v1

--- a/solution.py
+++ b/solution.py
@@ -74,7 +74,7 @@
             post_ref[(AT[i], 0) + at] = post[i]
         return carry
 
-    lax.fori_loop(0, (rows // 8) * tiles, body, 0)
+    lax.fori_loop(0, (rows // 8) * tiles, body, 0, unroll=2)
 
 
 def emit_halo(slot, last, edge, post_ref, fluid_ref, ys_ref, xs_ref, cs_ref):
@@ -118,7 +118,10 @@
         src_ref=src, dst_ref=dst, send_sem=send_sem, recv_sem=recv_sem, device_id=device, device_id_type=MESH)
 
 
-def halo_kernel(ys, xs, cs, yr, xr, cr, send_sem, recv_sem):
+def halo_kernel(noted, *refs):
+    ys, xs, cs = refs[:3]
+    yr, xr, cr = refs[3 + noted:6 + noted]
+    send_sem, recv_sem = refs[-2:]
     nz, nb = lax.axis_size("bz"), lax.axis_size("bxy")
     z, b = lax.axis_index("bz"), lax.axis_index("bxy")
 
@@ -134,9 +137,13 @@
               (xs.at[0], xr.at[0], 0, 1), (xs.at[1], xr.at[1], 0, -1)]
     for k, i in enumerate(CORNERS):
         routes.append((cs.at[k], cr.at[k], VELOCITIES[i][1], VELOCITIES[i][0]))
+    peers = [route[2:] for route in routes]
+    if noted:
+        note, from_left, from_right = refs[3], refs[7], refs[8]
+        routes += [(note, from_left, 0, 1), (note, from_right, 0, -1)]
     barrier = pltpu.get_barrier_semaphore()
     count = 0
-    for _s, _d, dz, db in routes:
+    for dz, db in peers:
         count = count + there(dz, db).astype(jnp.int32)
 
         @pl.when(there(dz, db))
@@ -159,18 +166,22 @@
             remote(src, dst, send_sem.at[n], recv_sem.at[n], (z - dz, b - db)).wait_recv()
 
 
-def exchange(ys, xs, cs):
-    vmem = pl.BlockSpec(memory_space=pltpu.VMEM)
+def exchange(ys, xs, cs, note=None):
+    hbm = pl.BlockSpec(memory_space=pl.ANY)
+    noted = note is not None
+    sent = [ys, xs, cs] + ([note] if noted else [])
+    got = sent + ([note] if noted else [])
+    count = 8 + 2 * noted
     return pl.pallas_call(
-        halo_kernel,
-        out_shape=[jax.ShapeDtypeStruct(a.shape, a.dtype) for a in (ys, xs, cs)],
-        in_specs=[vmem] * 3,
-        out_specs=[vmem] * 3,
-        scratch_shapes=[pltpu.SemaphoreType.DMA((8,)), pltpu.SemaphoreType.DMA((8,))],
-        compiler_params=pltpu.CompilerParams(collective_id=0, has_side_effects=True,
-                                             vmem_limit_bytes=8 * 1024 * 1024),
-        name="halo",
-    )(ys, xs, cs)
+        functools.partial(halo_kernel, int(noted)),
+        out_shape=[jax.ShapeDtypeStruct(a.shape, a.dtype) for a in got],
+        in_specs=[hbm] * len(sent),
+        out_specs=[hbm] * len(got),
+        scratch_shapes=[pltpu.SemaphoreType.DMA((count,)), pltpu.SemaphoreType.DMA((count,))],
+        compiler_params=pltpu.CompilerParams(collective_id=0 if noted else 2, has_side_effects=True,
+                                             vmem_limit_bytes=VMEM_LIMIT),
+        name="halo_noted" if noted else "halo",
+    )(*sent)
 
 
 def lane_shift(velocity, slot, edge, here, below, above, beside):
@@ -405,54 +416,53 @@
 
 def place(final, left, right, table):
     q, blocks, rows, width = final.shape
-    block = (q, 1, rows, width)
+    parts = 2 if rows % 16 == 0 else 1
+    block = (q, 1, rows // parts, width)
 
     def taken(kind):
-        return pl.BlockSpec(block, lambda k, table: (0, table[kind, k], 0, 0))
+        return pl.BlockSpec(
+            block, lambda k, h, table: (0, table[kind, k], jnp.where(table[3, k] == kind, h, parts - 1), 0))
 
     return pl.pallas_call(
         place_kernel,
         out_shape=jax.ShapeDtypeStruct(final.shape, final.dtype),
         grid_spec=pltpu.PrefetchScalarGridSpec(
-            num_scalar_prefetch=1, grid=(blocks,),
+            num_scalar_prefetch=1, grid=(blocks, parts),
             in_specs=[taken(0), taken(1), taken(2)],
-            out_specs=pl.BlockSpec(block, lambda k, table: (0, k, 0, 0))),
+            out_specs=pl.BlockSpec(block, lambda k, h, table: (0, k, h, 0))),
         compiler_params=pltpu.CompilerParams(vmem_limit_bytes=VMEM_LIMIT),
         name="place",
     )(table, final, left, right)
 
 
-def from_behind(value, axis, steps):
-    count = lax.axis_size(axis)
-    leading, last = (max(0, -steps), min(count, count - steps))
-    return lax.ppermute(value, axis, [(source, source + steps) for source in range(leading, last)])
-
-
-def routes_of(targets, blocks):
-    here = lax.axis_index("bxy")
-    goal = targets.reshape((blocks,))
-    left = from_behind(goal + 1, "bxy", 1) - 1
-    right = from_behind(goal + 1, "bxy", -1) - 1
+def arrivals(goal, left, right):
+    blocks = goal.shape[0]
+    here, owners = lax.axis_index("bxy"), lax.axis_size("bxy")
     numbers = jnp.arange(blocks, dtype=jnp.int32)
 
     def rank(going):
         return jnp.sum((going[None, :] & (numbers[None, :] < numbers[:, None])).astype(jnp.int32), axis=1)
 
-    def reaching(whose, from_index):
-        going = (whose // blocks == here) & (whose >= 0)
+    def reaching(whose, valid, from_index):
+        going = (whose // blocks == here) & valid
         hit = going[:, None] & (whose[:, None] - here * blocks == numbers[None, :])
         return jnp.any(hit, axis=0), jnp.sum(jnp.where(hit, from_index(going)[:, None], 0), axis=0)
 
-    is_left, left_index = reaching(left, rank)
-    is_right, right_index = reaching(right, rank)
+    is_left, left_index = reaching(left, here > 0, rank)
+    is_right, right_index = reaching(right, here < owners - 1, rank)
     kind = jnp.where(is_left, 1, jnp.where(is_right, 2, 0))
     index = jnp.where(is_left, left_index, jnp.where(is_right, right_index, numbers))
     used = kind[None, :, None] == jnp.arange(3, dtype=jnp.int32)[:, None, None]
     before = used & (numbers[:, None] <= numbers[None, :])[None]
     latest = jnp.max(jnp.where(before, numbers[None, :, None], -1), axis=1)
     held = jnp.sum(jnp.where(numbers[None, :, None] == latest[:, None, :], index[None, :, None], 0), axis=1)
-    table = jnp.concatenate([held, kind[None]], axis=0).astype(jnp.int32)
-
+    return jnp.concatenate([held, kind[None]], axis=0).astype(jnp.int32)
+
+
+def departures(goal):
+    blocks = goal.shape[0]
+    here = lax.axis_index("bxy")
+    numbers = jnp.arange(blocks, dtype=jnp.int32)
     way = jnp.where(goal // blocks == here + 1, 0, jnp.where(goal // blocks == here - 1, 1, 2))
     key = way * blocks + numbers
     place_of = jnp.sum((key[None, :] < key[:, None]).astype(jnp.int32), axis=1)
@@ -463,20 +473,21 @@
         return jnp.sum(jnp.where(place_of[:, None] == positions[None, :], values[:, None], 0), axis=0)
 
     stays = jnp.minimum(jnp.maximum(numbers, rights + lefts), blocks - 1)
-    plan = jnp.stack([
+    return jnp.stack([
         in_order(numbers, numbers), in_order(way, numbers),
         jnp.minimum(numbers, jnp.maximum(rights - 1, 0)),
         jnp.maximum(jnp.minimum(numbers - rights, lefts - 1), 0),
         in_order(goal % blocks, stays),
     ]).astype(jnp.int32)
-    return plan, table
 
 
 def on_device(pdfs, relax, fluid, targets):
     q, blocks, rows, width = pdfs.shape
     edge = rows
     f32 = jnp.float32
-    plan, table = routes_of(targets, blocks)
+    goal = targets.reshape((blocks,))
+    plan = departures(goal)
+    note = jnp.broadcast_to(jnp.pad(goal, (0, 128 - blocks))[None], (8, 128))
     here, row = lax.axis_index("bxy"), lax.axis_index("bz")
     ends = jnp.stack([here == 0, here == lax.axis_size("bxy") - 1, row == 0,
                       row == lax.axis_size("bz") - 1]).astype(jnp.int32)
@@ -500,7 +511,7 @@
         out_shape=[big] + halo_out, in_specs=[full, cell, cell],
         out_specs=[full, y_spec, x_spec, c_spec], compiler_params=params, name="first",
     )(pdfs, relax, fluid)
-    halo = exchange(ys, xs, cs)
+    *halo, left_goal, right_goal = exchange(ys, xs, cs, note)
     post, mask, ys, xs, cs = pl.pallas_call(
         functools.partial(middle_kernel, edge), grid=(blocks,),
         out_shape=[big, jax.ShapeDtypeStruct(fluid.shape, jnp.int32)] + halo_out,
@@ -536,6 +547,7 @@
         compiler_params=params, name="last",
     )(plan, mask, post, post, post, *halo)
     from_left, from_right = migrate(right, left)
+    table = arrivals(goal, left_goal[0, :blocks], right_goal[0, :blocks])
     return place(kept, from_left, from_right, table)
 
 

time: 177 us -> 167 us (0.944)
  local copies, waits for them, and re-layouts: 9.74 us -> 1.86 us
  starting transfers between devices: 6.42 us -> 0 us
  Pallas kernels: 153 us -> 155 us
  other arithmetic: 4.44 us -> 6.43 us
    unnamed x24 -> x0, local copies, waits for them, and re-layouts: 9.13 us -> none
    ppermute x2 -> x0, starting transfers between devices: 6.42 us -> none  [from_behind(): lax.ppermute(value, axis, [(source, source + steps) for source in range(l...]
  transfers between devices with their start and end apart: 2 -> 0, of which waited for: 0 -> 0; matrix products, arithmetic and copies ran while one was open for 2% -> 0% of each run, Pallas kernels for 81% -> 0%
where the time goes in v2:
time: 167 us
  Pallas kernels  155 us (93%)
  other arithmetic  6.43 us (4%)
  between operations  2.75 us (2%)
  local copies, waits for them, and re-layouts  1.86 us (1%)
    pallas_call x1, Pallas kernels, migrate(): pl.pallas_call(migrate_kernel, out_shape=[shape] * 3, in_specs=[hbm] * 2,...  84.9 us
    pallas_call x1, Pallas kernels, on_device(): pl.pallas_call(functools.partial(middle_kernel, edge), grid=(blocks,), ou...  18.5 us
    pallas_call x2, Pallas kernels, exchange(): pl.pallas_call(functools.partial(halo_kernel, int(noted)), out_shape=[jax...  16.5 us
    pallas_call x1, Pallas kernels, on_device(): pl.pallas_call(functools.partial(last_kernel, edge), out_shape=[sent, sen...  13.6 us
    pallas_call x1, Pallas kernels, place(): pl.pallas_call(place_kernel, out_shape=jax.ShapeDtypeStruct(final.shape,...  11.4 us
    pallas_call x1, Pallas kernels, on_device(): pl.pallas_call(functools.partial(first_kernel, edge), grid=(blocks,), out...  10.6 us

profile of v2, /device:TPU:1, one launch (start us, length us, event | category | flops | bytes accessed | tf_op | source)
XLA Modules:
  0.0 166.5 jit_solution(7763998006444200701)
XLA Ops:
  0.0 0.6 add_convert_fusion.ends_ref
  0.6 0.7 pad.4
  1.2 0.7 iota_add_fusion
  1.9 0.2 convert_reduce_fusion
  2.1 0.7 fusion.7
  5.5 0.7 minimum_maximum_fusion
  6.2 0.1 select_reduce_fusion.2
  6.3 0.6 stack.32.plan_ref
  6.9 0.6 broadcast_in_dim.104.refs_3_
  7.5 10.6 %first.1 = (f32[19,4,32,1024]{3,2,1,0:T(8,128)}, f32[2,6,32,128]{3,2,1,0:T(8,128)}, f32[2,4,8,1024]{3,2,1,0:T(8,128)}, f32[4,8,128]{2,1,0:T(8,128)}) custom-call(f32[19,4,32,1024]{3,2,1,0:T(8,128)} %pdfs_ref.1, f32[4,32,1024]{2,1,0:T(8,128)} %relax_ref.3, s32[4,32,1024]{2,1,0:T(8,128)} %fabove_ref.1), custom_call_target="tpu_custom_call" | custom-call | tf_op jit(solution)/shard_map/first/pallas_call | solution.py:509
  18.1 8.8 %halo_noted.1 = (f32[2,6,32,128]{3,2,1,0:T(8,128)}, f32[2,4,8,1024]{3,2,1,0:T(8,128)}, f32[4,8,128]{2,1,0:T(8,128)}, s32[8,128]{1,0:T(8,128)}, s32[8,128]{1,0:T(8,128)}) custom-call(f32[2,6,32,128]{3,2,1,0:T(8,128)} %get-tuple-element.27.refs_0_, f32[2,4,8,1024]{3,2,1,0:T(8,128)} %get-tuple-element.28.refs_1_, f32[4,8,128]{2,1,0:T(8,128)} %get-tuple-element.29.refs_2_, ...), custom_call_target="tpu_custom_call" | custom-call | tf_op jit(solution)/shard_map/halo_noted/pallas_call | solution.py:175
  26.9 0.7 bitcast_subtract_fusion
  27.5 0.7 and_bitcast_fusion
  28.2 0.7 compare_and_fusion
  28.9 0.1 convert_reduce_fusion.1
  29.1 0.1 select_reduce_fusion.5
  29.2 0.1 fusion.4
  29.2 0.1 convert_reduce_fusion.2
  29.4 0.1 select_reduce_fusion.6
  29.5 0.1 fusion.5
  29.6 0.1 select_reduce_fusion.1
  29.7 0.1 select_reduce_fusion
  29.7 0.6 pad_add_fusion.table_ref
  30.4 18.5 %middle.1 = (f32[19,4,32,1024]{3,2,1,0:T(8,128)}, s32[4,32,1024]{2,1,0:T(8,128)}, f32[2,6,32,128]{3,2,1,0:T(8,128)}, f32[2,4,8,1024]{3,2,1,0:T(8,128)}, f32[4,8,128]{2,1,0:T(8,128)}) custom-call(s32[4]{0:T(128)} %add_convert_fusion.ends_ref, f32[19,4,32,1024]{3,2,1,0:T(8,128)} %get-tuple-element.32.post_ref.below_ref.above_ref, ...), custom_call_target="tpu_custom_call" | custom-call | tf_op jit(solution)/shard_map/middle/pallas_call | solution.py:515
  48.9 7.7 %halo.1 = (f32[2,6,32,128]{3,2,1,0:T(8,128)}, f32[2,4,8,1024]{3,2,1,0:T(8,128)}, f32[4,8,128]{2,1,0:T(8,128)}) custom-call(f32[2,6,32,128]{3,2,1,0:T(8,128)} %get-tuple-element.38.refs_0_, f32[2,4,8,1024]{3,2,1,0:T(8,128)} %get-tuple-element.39.refs_1_, f32[4,8,128]{2,1,0:T(8,128)} %get-tuple-element.40.refs_2_), custom_call_target="tpu_custom_call" | custom-call | tf_op jit(solution)/shard_map/halo/pallas_call | solution.py:175
  56.6 13.6 %last.1 = (f32[19,2,32,1024]{3,2,1,0:T(8,128)}, f32[19,2,32,1024]{3,2,1,0:T(8,128)}, f32[19,4,32,1024]{3,2,1,0:T(8,128)}) custom-call(s32[5,4]{1,0:T(8,128)} %stack.32.plan_ref, s32[4,32,1024]{2,1,0:T(8,128)} %get-tuple-element.36.mask_ref, f32[19,4,32,1024]{3,2,1,0:T(8,128)} %get-tuple-element.37.post_ref.below_ref.above_ref, ...), custom_call_target="tpu_custom_call" | custom-call | tf_op jit(solution)/shard_map/last/pallas_call | solution.py:539
  70.2 84.9 %migrate.1 = (f32[19,2,32,1024]{3,2,1,0:T(8,128)}, f32[19,2,32,1024]{3,2,1,0:T(8,128)}, f32[19,2,32,1024]{3,2,1,0:T(8,128)}) custom-call(f32[19,2,32,1024]{3,2,1,0:T(8,128)} %get-tuple-element.45.right, f32[19,2,32,1024]{3,2,1,0:T(8,128)} %get-tuple-element.46.left), custom_call_target="tpu_custom_call" | custom-call | tf_op jit(solution)/shard_map/migrate/pallas_call | solution.py:392
  155.1 11.4 %place.1 = f32[19,4,32,1024]{3,2,1,0:T(8,128)} custom-call(s32[4,4]{1,0:T(4,128)} %pad_add_fusion.table_ref, f32[19,4,32,1024]{3,2,1,0:T(8,128)} %get-tuple-element.44.final_ref, f32[19,2,32,1024]{3,2,1,0:T(8,128)} %get-tuple-element.47.left_ref, f32[19,2,32,1024]{3,2,1,0:T(8,128)} %get-tuple-element.48.right_ref), custom_call_target="tpu_custom_call" | custom-call | tf_op jit(solution)/shard_map/place/pallas_call | solution.py:426
  (4 shorter events, 0.0 us)

commit v3 on v2

--- a/solution.py
+++ b/solution.py
@@ -254,13 +254,15 @@
         write(i, jnp.where((mask & (1 << i)) != 0, value, stay))
 
 
-def middle_kernel(edge, ends_ref, post_ref, below_ref, above_ref, relax_ref, fluid_ref, fbelow_ref, fabove_ref,
+def middle_kernel(edge, post_ref, below_ref, above_ref, relax_ref, fluid_ref, fbelow_ref, fabove_ref,
                   yr_ref, xr_ref, cr_ref, out_ref, mask_ref, ys_ref, xs_ref, cs_ref, next_ref):
     slot, slots = pl.program_id(0), pl.num_programs(0)
     rows, width = fluid_ref.shape[1:]
     row = lax.broadcasted_iota(jnp.int32, (rows, width), 0)
     lane = lax.broadcasted_iota(jnp.int32, (rows, width), 1)
     depth = lane % edge
+    z, b = lax.axis_index("bz"), lax.axis_index("bxy")
+    at_end = (b == 0, b == lax.axis_size("bxy") - 1, z == 0, z == lax.axis_size("bz") - 1)
     fluid = fluid_ref[0].astype(jnp.float32)
     bits = jnp.ones((rows, width), jnp.int32)
     for i in range(1, Q):
@@ -270,10 +272,10 @@
         bit = jnp.where(source > 0.5, 1 << i, 0)
         if cx:
             edge_row = 0 if cx == 1 else rows - 1
-            bit = jnp.where((row == edge_row) & (ends_ref[0 if cx == 1 else 1] > 0), 0, bit)
+            bit = jnp.where((row == edge_row) & at_end[0 if cx == 1 else 1], 0, bit)
         if cy:
             outer = lane < edge if cy == 1 else lane >= width - edge
-            bit = jnp.where(outer & (ends_ref[2 if cy == 1 else 3] > 0), 0, bit)
+            bit = jnp.where(outer & at_end[2 if cy == 1 else 3], 0, bit)
         if cz:
             final = 0 if cz == 1 else slots - 1
             face = 0 if cz == 1 else edge - 1
@@ -416,7 +418,7 @@
 
 def place(final, left, right, table):
     q, blocks, rows, width = final.shape
-    parts = 2 if rows % 16 == 0 else 1
+    parts = 1
     block = (q, 1, rows // parts, width)
 
     def taken(kind):
@@ -435,62 +437,66 @@
     )(table, final, left, right)
 
 
-def arrivals(goal, left, right):
-    blocks = goal.shape[0]
+def tables_kernel(goal_ref, left_ref, right_ref, plan_ref, table_ref):
     here, owners = lax.axis_index("bxy"), lax.axis_size("bxy")
-    numbers = jnp.arange(blocks, dtype=jnp.int32)
-
-    def rank(going):
-        return jnp.sum((going[None, :] & (numbers[None, :] < numbers[:, None])).astype(jnp.int32), axis=1)
-
-    def reaching(whose, valid, from_index):
-        going = (whose // blocks == here) & valid
-        hit = going[:, None] & (whose[:, None] - here * blocks == numbers[None, :])
-        return jnp.any(hit, axis=0), jnp.sum(jnp.where(hit, from_index(going)[:, None], 0), axis=0)
-
-    is_left, left_index = reaching(left, here > 0, rank)
-    is_right, right_index = reaching(right, here < owners - 1, rank)
-    kind = jnp.where(is_left, 1, jnp.where(is_right, 2, 0))
-    index = jnp.where(is_left, left_index, jnp.where(is_right, right_index, numbers))
-    used = kind[None, :, None] == jnp.arange(3, dtype=jnp.int32)[:, None, None]
-    before = used & (numbers[:, None] <= numbers[None, :])[None]
-    latest = jnp.max(jnp.where(before, numbers[None, :, None], -1), axis=1)
-    held = jnp.sum(jnp.where(numbers[None, :, None] == latest[:, None, :], index[None, :, None], 0), axis=1)
-    return jnp.concatenate([held, kind[None]], axis=0).astype(jnp.int32)
-
-
-def departures(goal):
-    blocks = goal.shape[0]
-    here = lax.axis_index("bxy")
-    numbers = jnp.arange(blocks, dtype=jnp.int32)
-    way = jnp.where(goal // blocks == here + 1, 0, jnp.where(goal // blocks == here - 1, 1, 2))
-    key = way * blocks + numbers
-    place_of = jnp.sum((key[None, :] < key[:, None]).astype(jnp.int32), axis=1)
-    rights = jnp.sum((way == 0).astype(jnp.int32))
-    lefts = jnp.sum((way == 1).astype(jnp.int32))
-
-    def in_order(values, positions):
-        return jnp.sum(jnp.where(place_of[:, None] == positions[None, :], values[:, None], 0), axis=0)
-
-    stays = jnp.minimum(jnp.maximum(numbers, rights + lefts), blocks - 1)
-    return jnp.stack([
-        in_order(numbers, numbers), in_order(way, numbers),
-        jnp.minimum(numbers, jnp.maximum(rights - 1, 0)),
-        jnp.maximum(jnp.minimum(numbers - rights, lefts - 1), 0),
-        in_order(goal % blocks, stays),
-    ]).astype(jnp.int32)
+    blocks = goal_ref.shape[2]
+    base = here * blocks
+
+    def total(terms):
+        return sum(t.astype(jnp.int32) for t in terms)
+
+    goal = [goal_ref[0, 0, j] for j in range(blocks)]
+    way = [jnp.where(g >= base + blocks, 0, jnp.where(g < base, 1, 2)) for g in goal]
+    key = [way[j] * blocks + j for j in range(blocks)]
+    at = [total(key[k] < key[j] for k in range(blocks)) for j in range(blocks)]
+    rights, lefts = total(w == 0 for w in way), total(w == 1 for w in way)
+
+    def in_order(values, position):
+        return sum(jnp.where(at[j] == position, values[j], 0) for j in range(blocks))
+
+    for g in range(blocks):
+        plan_ref[0, g] = in_order(list(range(blocks)), g)
+        plan_ref[1, g] = in_order(way, g)
+        plan_ref[2, g] = jnp.minimum(g, jnp.maximum(rights - 1, 0))
+        plan_ref[3, g] = jnp.maximum(jnp.minimum(g - rights, lefts - 1), 0)
+        first = jnp.minimum(jnp.maximum(g, rights + lefts), blocks - 1)
+        plan_ref[4, g] = in_order([lax.rem(v, blocks) for v in goal], first)
+
+    kind = [jnp.int32(0)] * blocks
+    index = [jnp.int32(k) for k in range(blocks)]
+    for source, ref, valid in ((1, left_ref, here > 0), (2, right_ref, here < owners - 1)):
+        rank = jnp.int32(0)
+        for j in range(blocks):
+            value = ref[j, 0]
+            for k in range(blocks):
+                hit = valid & (value == base + k)
+                kind[k] = jnp.where(hit, source, kind[k])
+                index[k] = jnp.where(hit, rank, index[k])
+            rank = rank + (valid & (value >= base) & (value < base + blocks)).astype(jnp.int32)
+    for source in range(3):
+        held = jnp.int32(0)
+        for k in range(blocks):
+            held = jnp.where(kind[k] == source, index[k], held)
+            table_ref[source, k] = held
+    for k in range(blocks):
+        table_ref[3, k] = kind[k]
+
+
+def tables(targets, left_goal, right_goal):
+    blocks = targets.shape[2]
+    smem = pl.BlockSpec(memory_space=pltpu.SMEM)
+    return pl.pallas_call(
+        tables_kernel,
+        out_shape=[jax.ShapeDtypeStruct((5, blocks), jnp.int32), jax.ShapeDtypeStruct((4, blocks), jnp.int32)],
+        in_specs=[smem] * 3, out_specs=[smem] * 2, name="tables",
+    )(targets, left_goal, right_goal)
 
 
 def on_device(pdfs, relax, fluid, targets):
     q, blocks, rows, width = pdfs.shape
     edge = rows
     f32 = jnp.float32
-    goal = targets.reshape((blocks,))
-    plan = departures(goal)
-    note = jnp.broadcast_to(jnp.pad(goal, (0, 128 - blocks))[None], (8, 128))
-    here, row = lax.axis_index("bxy"), lax.axis_index("bz")
-    ends = jnp.stack([here == 0, here == lax.axis_size("bxy") - 1, row == 0,
-                      row == lax.axis_size("bz") - 1]).astype(jnp.int32)
+    note = jnp.broadcast_to(targets.reshape((blocks, 1)), (blocks, 128))
     full = pl.BlockSpec((q, 1, rows, width), lambda s: (0, s, 0, 0))
     cell = pl.BlockSpec((1, rows, width), lambda s: (s, 0, 0))
     cell_below = pl.BlockSpec((1, rows, width), lambda s: (jnp.maximum(s - 1, 0), 0, 0))
@@ -512,14 +518,15 @@
         out_specs=[full, y_spec, x_spec, c_spec], compiler_params=params, name="first",
     )(pdfs, relax, fluid)
     *halo, left_goal, right_goal = exchange(ys, xs, cs, note)
+    plan, table = tables(targets, left_goal, right_goal)
     post, mask, ys, xs, cs = pl.pallas_call(
         functools.partial(middle_kernel, edge), grid=(blocks,),
         out_shape=[big, jax.ShapeDtypeStruct(fluid.shape, jnp.int32)] + halo_out,
-        in_specs=[pl.BlockSpec(memory_space=pltpu.SMEM), full, below, above, cell, cell, cell_below, cell_above,
+        in_specs=[full, below, above, cell, cell, cell_below, cell_above,
                   y_spec, x_all, c_spec],
         out_specs=[full, cell, y_spec, x_spec, c_spec],
         scratch_shapes=[pltpu.VMEM((q, rows, width), f32)], compiler_params=params, name="middle",
-    )(ends, post, post, post, relax, fluid, fluid, fluid, *halo)
+    )(post, post, post, relax, fluid, fluid, fluid, *halo)
     halo = exchange(ys, xs, cs)
     def moved(spec, shift):
         shape = spec.block_shape
@@ -547,7 +554,6 @@
         compiler_params=params, name="last",
     )(plan, mask, post, post, post, *halo)
     from_left, from_right = migrate(right, left)
-    table = arrivals(goal, left_goal[0, :blocks], right_goal[0, :blocks])
     return place(kept, from_left, from_right, table)
 
 

time: 167 us -> 157 us (0.940)
  other arithmetic: 6.43 us -> 0 us
  between operations: 2.75 us -> 0.04 us
where the time goes in v3:
time: 157 us
  Pallas kernels  156 us (99%)
    pallas_call x1, Pallas kernels, migrate(): pl.pallas_call(migrate_kernel, out_shape=[shape] * 3, in_specs=[hbm] * 2,...  85 us
    pallas_call x1, Pallas kernels, on_device(): pl.pallas_call(functools.partial(middle_kernel, edge), grid=(blocks,), ou...  18.5 us
    pallas_call x2, Pallas kernels, exchange(): pl.pallas_call(functools.partial(halo_kernel, int(noted)), out_shape=[jax...  16.4 us
    pallas_call x1, Pallas kernels, on_device(): pl.pallas_call(functools.partial(last_kernel, edge), out_shape=[sent, sen...  13.7 us
    pallas_call x1, Pallas kernels, on_device(): pl.pallas_call(functools.partial(first_kernel, edge), grid=(blocks,), out...  10.6 us
    pallas_call x1, Pallas kernels, place(): pl.pallas_call(place_kernel, out_shape=jax.ShapeDtypeStruct(final.shape,...  9.94 us

profile of v3, /device:TPU:1, one launch (start us, length us, event | category | flops | bytes accessed | tf_op | source)
XLA Modules:
  0.0 156.9 jit_solution(8011739532531850583)
XLA Ops:
  0.0 1.3 broadcast_in_dim.8.refs_3_
  1.3 10.6 %first.1 = (f32[19,4,32,1024]{3,2,1,0:T(8,128)}, f32[2,6,32,128]{3,2,1,0:T(8,128)}, f32[2,4,8,1024]{3,2,1,0:T(8,128)}, f32[4,8,128]{2,1,0:T(8,128)}) custom-call(f32[19,4,32,1024]{3,2,1,0:T(8,128)} %pdfs_ref.1, f32[4,32,1024]{2,1,0:T(8,128)} %relax_ref.3, s32[4,32,1024]{2,1,0:T(8,128)} %fabove_ref.1), custom_call_target="tpu_custom_call" | custom-call | tf_op jit(solution)/shard_map/first/pallas_call | solution.py:515
  11.8 8.8 %halo_noted.1 = (f32[2,6,32,128]{3,2,1,0:T(8,128)}, f32[2,4,8,1024]{3,2,1,0:T(8,128)}, f32[4,8,128]{2,1,0:T(8,128)}, s32[4,128]{1,0:T(4,128)}, s32[4,128]{1,0:T(4,128)}) custom-call(f32[2,6,32,128]{3,2,1,0:T(8,128)} %get-tuple-element.29.refs_0_, f32[2,4,8,1024]{3,2,1,0:T(8,128)} %get-tuple-element.30.refs_1_, f32[4,8,128]{2,1,0:T(8,128)} %get-tuple-element.31.refs_2_, ...), custom_call_target="tpu_custom_call" | custom-call | tf_op jit(solution)/shard_map/halo_noted/pallas_call | solution.py:175
  20.6 1.5 tables.1
  22.1 18.5 %middle.1 = (f32[19,4,32,1024]{3,2,1,0:T(8,128)}, s32[4,32,1024]{2,1,0:T(8,128)}, f32[2,6,32,128]{3,2,1,0:T(8,128)}, f32[2,4,8,1024]{3,2,1,0:T(8,128)}, f32[4,8,128]{2,1,0:T(8,128)}) custom-call(f32[19,4,32,1024]{3,2,1,0:T(8,128)} %get-tuple-element.36.post_ref.below_ref.above_ref, f32[19,4,32,1024]{3,2,1,0:T(8,128)} %get-tuple-element.36.post_ref.below_ref.above_ref, ...), custom_call_target="tpu_custom_call" | custom-call | tf_op jit(solution)/shard_map/middle/pallas_call | solution.py:522
  40.6 7.7 %halo.1 = (f32[2,6,32,128]{3,2,1,0:T(8,128)}, f32[2,4,8,1024]{3,2,1,0:T(8,128)}, f32[4,8,128]{2,1,0:T(8,128)}) custom-call(f32[2,6,32,128]{3,2,1,0:T(8,128)} %get-tuple-element.42.refs_0_, f32[2,4,8,1024]{3,2,1,0:T(8,128)} %get-tuple-element.43.refs_1_, f32[4,8,128]{2,1,0:T(8,128)} %get-tuple-element.44.refs_2_), custom_call_target="tpu_custom_call" | custom-call | tf_op jit(solution)/shard_map/halo/pallas_call | solution.py:175
  48.3 13.7 %last.1 = (f32[19,2,32,1024]{3,2,1,0:T(8,128)}, f32[19,2,32,1024]{3,2,1,0:T(8,128)}, f32[19,4,32,1024]{3,2,1,0:T(8,128)}) custom-call(s32[5,4]{1,0:T(8,128)} %get-tuple-element.35.plan_ref, s32[4,32,1024]{2,1,0:T(8,128)} %get-tuple-element.40.mask_ref, f32[19,4,32,1024]{3,2,1,0:T(8,128)} %get-tuple-element.41.post_ref.below_ref.above_ref, ...), custom_call_target="tpu_custom_call" | custom-call | tf_op jit(solution)/shard_map/last/pallas_call | solution.py:546
  62.0 85.0 %migrate.1 = (f32[19,2,32,1024]{3,2,1,0:T(8,128)}, f32[19,2,32,1024]{3,2,1,0:T(8,128)}, f32[19,2,32,1024]{3,2,1,0:T(8,128)}) custom-call(f32[19,2,32,1024]{3,2,1,0:T(8,128)} %get-tuple-element.49.right, f32[19,2,32,1024]{3,2,1,0:T(8,128)} %get-tuple-element.50.left), custom_call_target="tpu_custom_call" | custom-call | tf_op jit(solution)/shard_map/migrate/pallas_call | solution.py:394
  147.0 9.9 %place.1 = f32[19,4,32,1024]{3,2,1,0:T(8,128)} custom-call(s32[4,4]{1,0:T(4,128)} %get-tuple-element.34.table_ref, f32[19,4,32,1024]{3,2,1,0:T(8,128)} %get-tuple-element.48.final_ref, f32[19,2,32,1024]{3,2,1,0:T(8,128)} %get-tuple-element.51.left_ref, f32[19,2,32,1024]{3,2,1,0:T(8,128)} %get-tuple-element.52.right_ref), custom_call_target="tpu_custom_call" | custom-call | tf_op jit(solution)/shard_map/place/pallas_call | solution.py:428

commit v4 on v3

--- a/solution.py
+++ b/solution.py
@@ -74,7 +74,7 @@
             post_ref[(AT[i], 0) + at] = post[i]
         return carry
 
-    lax.fori_loop(0, (rows // 8) * tiles, body, 0, unroll=2)
+    lax.fori_loop(0, (rows // 8) * tiles, body, 0, unroll=4)
 
 
 def emit_halo(slot, last, edge, post_ref, fluid_ref, ys_ref, xs_ref, cs_ref):

time: 157 us -> 156 us (level)
  no operation moved by 1% of the time
where the time goes in v4:
time: 156 us
  Pallas kernels  155 us (99%)
    pallas_call x1, Pallas kernels, migrate(): pl.pallas_call(migrate_kernel, out_shape=[shape] * 3, in_specs=[hbm] * 2,...  85.6 us
    pallas_call x1, Pallas kernels, on_device(): pl.pallas_call(functools.partial(middle_kernel, edge), grid=(blocks,), ou...  18.2 us
    pallas_call x2, Pallas kernels, exchange(): pl.pallas_call(functools.partial(halo_kernel, int(noted)), out_shape=[jax...  16.4 us
    pallas_call x1, Pallas kernels, on_device(): pl.pallas_call(functools.partial(last_kernel, edge), out_shape=[sent, sen...  12.8 us
    pallas_call x1, Pallas kernels, on_device(): pl.pallas_call(functools.partial(first_kernel, edge), grid=(blocks,), out...  10.4 us
    pallas_call x1, Pallas kernels, place(): pl.pallas_call(place_kernel, out_shape=jax.ShapeDtypeStruct(final.shape,...  9.95 us

profile of v4, /device:TPU:1, one launch (start us, length us, event | category | flops | bytes accessed | tf_op | source)
XLA Modules:
  0.0 156.1 jit_solution(13342311321948833696)
XLA Ops:
  0.0 1.3 broadcast_in_dim.8.refs_3_
  1.3 10.4 %first.1 = (f32[19,4,32,1024]{3,2,1,0:T(8,128)}, f32[2,6,32,128]{3,2,1,0:T(8,128)}, f32[2,4,8,1024]{3,2,1,0:T(8,128)}, f32[4,8,128]{2,1,0:T(8,128)}) custom-call(f32[19,4,32,1024]{3,2,1,0:T(8,128)} %pdfs_ref.1, f32[4,32,1024]{2,1,0:T(8,128)} %relax_ref.3, s32[4,32,1024]{2,1,0:T(8,128)} %fabove_ref.1), custom_call_target="tpu_custom_call" | custom-call | tf_op jit(solution)/shard_map/first/pallas_call | solution.py:515
  11.6 8.8 %halo_noted.1 = (f32[2,6,32,128]{3,2,1,0:T(8,128)}, f32[2,4,8,1024]{3,2,1,0:T(8,128)}, f32[4,8,128]{2,1,0:T(8,128)}, s32[4,128]{1,0:T(4,128)}, s32[4,128]{1,0:T(4,128)}) custom-call(f32[2,6,32,128]{3,2,1,0:T(8,128)} %get-tuple-element.29.refs_0_, f32[2,4,8,1024]{3,2,1,0:T(8,128)} %get-tuple-element.30.refs_1_, f32[4,8,128]{2,1,0:T(8,128)} %get-tuple-element.31.refs_2_, ...), custom_call_target="tpu_custom_call" | custom-call | tf_op jit(solution)/shard_map/halo_noted/pallas_call | solution.py:175
  20.4 1.5 tables.1
  21.9 18.2 %middle.1 = (f32[19,4,32,1024]{3,2,1,0:T(8,128)}, s32[4,32,1024]{2,1,0:T(8,128)}, f32[2,6,32,128]{3,2,1,0:T(8,128)}, f32[2,4,8,1024]{3,2,1,0:T(8,128)}, f32[4,8,128]{2,1,0:T(8,128)}) custom-call(f32[19,4,32,1024]{3,2,1,0:T(8,128)} %get-tuple-element.36.post_ref.below_ref.above_ref, f32[19,4,32,1024]{3,2,1,0:T(8,128)} %get-tuple-element.36.post_ref.below_ref.above_ref, ...), custom_call_target="tpu_custom_call" | custom-call | tf_op jit(solution)/shard_map/middle/pallas_call | solution.py:522
  40.1 7.7 %halo.1 = (f32[2,6,32,128]{3,2,1,0:T(8,128)}, f32[2,4,8,1024]{3,2,1,0:T(8,128)}, f32[4,8,128]{2,1,0:T(8,128)}) custom-call(f32[2,6,32,128]{3,2,1,0:T(8,128)} %get-tuple-element.42.refs_0_, f32[2,4,8,1024]{3,2,1,0:T(8,128)} %get-tuple-element.43.refs_1_, f32[4,8,128]{2,1,0:T(8,128)} %get-tuple-element.44.refs_2_), custom_call_target="tpu_custom_call" | custom-call | tf_op jit(solution)/shard_map/halo/pallas_call | solution.py:175
  47.8 12.8 %last.1 = (f32[19,2,32,1024]{3,2,1,0:T(8,128)}, f32[19,2,32,1024]{3,2,1,0:T(8,128)}, f32[19,4,32,1024]{3,2,1,0:T(8,128)}) custom-call(s32[5,4]{1,0:T(8,128)} %get-tuple-element.35.plan_ref, s32[4,32,1024]{2,1,0:T(8,128)} %get-tuple-element.40.mask_ref, f32[19,4,32,1024]{3,2,1,0:T(8,128)} %get-tuple-element.41.post_ref.below_ref.above_ref, ...), custom_call_target="tpu_custom_call" | custom-call | tf_op jit(solution)/shard_map/last/pallas_call | solution.py:546
  60.6 85.6 %migrate.1 = (f32[19,2,32,1024]{3,2,1,0:T(8,128)}, f32[19,2,32,1024]{3,2,1,0:T(8,128)}, f32[19,2,32,1024]{3,2,1,0:T(8,128)}) custom-call(f32[19,2,32,1024]{3,2,1,0:T(8,128)} %get-tuple-element.49.right, f32[19,2,32,1024]{3,2,1,0:T(8,128)} %get-tuple-element.50.left), custom_call_target="tpu_custom_call" | custom-call | tf_op jit(solution)/shard_map/migrate/pallas_call | solution.py:394
  146.2 9.9 %place.1 = f32[19,4,32,1024]{3,2,1,0:T(8,128)} custom-call(s32[4,4]{1,0:T(4,128)} %get-tuple-element.34.table_ref, f32[19,4,32,1024]{3,2,1,0:T(8,128)} %get-tuple-element.48.final_ref, f32[19,2,32,1024]{3,2,1,0:T(8,128)} %get-tuple-element.51.left_ref, f32[19,2,32,1024]{3,2,1,0:T(8,128)} %get-tuple-element.52.right_ref), custom_call_target="tpu_custom_call" | custom-call | tf_op jit(solution)/shard_map/place/pallas_call | solution.py:428
